TPU v7x, 32 devices: a whole 2x2x4 slice. The times are simulated.
32 devices in a mesh: row: 2 (over core), col: 4 (over y, x), depth: 4 (over z).
Axes of the slice: x: 2, y: 2, z: 4, core: 2. Of those that a mesh axis runs over, the one named last changes fastest.
Arguments:
- head_rhs: float32 [2, 1024, 4096], P(None, 'row', ('col', 'depth')), may hold values from -6 to 6
- head_factor: float32 [1024, 1024], P('row', 'depth'), may hold values from -0.09375 to 0.09375
- inverses: float32 [2, 1024, 1024], P(None, 'depth'), as said below
- trail_factor: float32 [512, 2, 1024], P('row', None, 'depth'), may hold values from -0.125 to 0.125
- trail_rhs: float32 [512, 4096], P('row', ('col', 'depth')), may hold values from -6 to 6
Outputs:
- solution: float32 [2, 1024, 4096], P(None, 'depth', 'col')
- trail_out: float32 [512, 4096], P('row', ('col', 'depth'))
Inputs may be any that keep to these rules, and one draw needn't show every extreme that they name: `inverses`: each of the two blocks is lower triangular with a positive diagonal.
All inputs are finite; a program needn't handle non-finite values.
Results may differ from a plain program's by a relative error of at most 0.00009.
Values sent between devices are 32-bit elements; how exact they have to be, the bound alone decides.
No kernel may reach another device: no remote copies, remote signals or barrier semaphores. Data moves between devices by JAX's collectives and lax.ppermute only.
A program may use at most 64 MiB of HBM per device.

v0:
```python
import jax
import jax.numpy as jnp
from jax import lax
from jax.sharding import PartitionSpec as P


def product(left, right):
    return jnp.dot(left, right, precision=lax.Precision.HIGH, preferred_element_type=jnp.float32)


def exchange(value, axis, flip):
    size = lax.axis_size(axis)
    return lax.ppermute(value, axis, [(i, i ^ flip) for i in range(size)])


def in_order(blocks, index):
    bit = 1
    while bit < len(blocks):
        odd = (index & bit) != 0
        blocks = [jnp.where(odd, blocks[k ^ bit], blocks[k]) for k in range(len(blocks))]
        bit *= 2
    return blocks


def share_rows(value, dim):
    size = lax.axis_size("row")
    index = lax.axis_index("row")
    bit = 1
    while bit < size:
        other = exchange(value, "row", bit)
        odd = (index & bit) != 0
        value = jnp.concatenate([jnp.where(odd, other, value), jnp.where(odd, value, other)], axis=dim)
        bit *= 2
    return value


def own_part(value, dim, axis):
    size = value.shape[dim] // lax.axis_size(axis)
    return lax.dynamic_slice_in_dim(value, lax.axis_index(axis) * size, size, dim)


def from_depth(part):
    return jnp.stack([exchange(part, "depth", k) for k in range(1, lax.axis_size("depth"))])


def from_columns(parts, first):
    index = lax.axis_index("col")
    size = lax.axis_size("col")
    known = {0: parts}
    bits = []
    bit = 1
    while bit < size:
        bits.append(bit)
        bit *= 2
    for bit in bits:
        known[bit] = exchange(parts, "col", bit)
    order = bits if first else bits[::-1]
    for k in range(1, size):
        if k in known:
            continue
        last = [b for b in order if k & b][-1]
        known[k] = exchange(known[k ^ last], "col", last)
    return in_order([known[k] for k in range(size)], index)


def gather_factor(own, dim, first):
    parts = from_depth(own_part(own, dim, "col"))
    parts = from_columns(parts, first)
    rest = jnp.concatenate(parts, axis=dim + 1)
    return [own] + [rest[k] for k in range(rest.shape[0])]


def to_output(block_parts):
    arrived = [block_parts[0]] + [exchange(block_parts[k], "depth", k) for k in range(1, len(block_parts))]
    return jnp.concatenate(in_order(arrived, lax.axis_index("depth")), axis=1)


def steps(head_rhs, head_factor, inverses, trail_factor, trail_rhs):
    lower = own_part(inverses, 1, "row")
    first_inverse = gather_factor(lower[0], 0, True)
    factor = gather_factor(head_factor, 0, False)
    second_inverse = gather_factor(lower[1], 0, True)
    trail = gather_factor(trail_factor, 0, False)

    count = len(factor)
    rhs = share_rows(head_rhs[0], 0)
    first_parts = [product(piece, rhs) for piece in first_inverse]
    first_out = to_output(first_parts)
    first = share_rows(jnp.stack(first_parts), 1)
    change = sum(product(factor[k], first[k]) for k in range(count))
    second_rhs = share_rows(head_rhs[1] - change, 0)
    second_parts = [product(piece, second_rhs) for piece in second_inverse]
    second_out = to_output(second_parts)
    second = share_rows(jnp.stack(second_parts), 1)
    trail_out = trail_rhs - sum(product(trail[k][:, 0, :], first[k]) for k in range(count))
    trail_out = trail_out - sum(product(trail[k][:, 1, :], second[k]) for k in range(count))
    return share_rows(jnp.stack([first_out, second_out]), 1), trail_out


def solution(mesh):
    placed = (
        P(None, "row", ("col", "depth")),
        P("row", "depth"),
        P(None, "depth", None),
        P("row", None, "depth"),
        P("row", ("col", "depth")),
    )
    return jax.shard_map(
        steps,
        mesh=mesh,
        in_specs=placed,
        out_specs=(P(None, "depth", "col"), P("row", ("col", "depth"))),
        check_vma=False,
    )
```

profile of v0, /device:TPU:0, one launch (start us, length us, event | category | flops | bytes accessed | tf_op | source)
XLA Modules:
  0.0 137.1 jit_solution(2174089717334203335)
XLA Ops:
  2.3 3.1 %collective-permute-start.17 = (f32[128,256]{1,0:T(8,128)}, f32[128,256]{1,0:T(8,128)S(1)}, u32[]{:S(2)}, u32[]{:S(2)}) collective-permute-start(f32[128,256]{1,0:T(8,128)} %constant_dynamic-slice_fusion.1), channel_id=1, source_target_pairs={{0,1},{1,0},{2,3},{3,2},{4,5},{5,4},{6,7},{7,6},{8,9},{9,8},{10,11... | collective-permute-start | bytes 393224 | tf_op jit(solution)/shard_map/ppermute | solution.py:13
  5.4 2.6 %collective-permute-start.18 = (f32[128,256]{1,0:T(8,128)}, f32[128,256]{1,0:T(8,128)S(1)}, u32[]{:S(2)}, u32[]{:S(2)}) collective-permute-start(f32[128,256]{1,0:T(8,128)} %constant_dynamic-slice_fusion.1), channel_id=1, source_target_pairs={{0,2},{1,3},{2,0},{3,1},{4,6},{5,7},{6,4},{7,5},{8,10},{9,11},{10,... | collective-permute-start | bytes 393224 | tf_op jit(solution)/shard_map/ppermute | solution.py:13
  8.0 1.7 %dynamic-slice_bitcast_fusion.5 = (f32[32,1024]{1,0:T(8,128)}, f32[32,1024]{1,0:T(8,128)}) fusion(f32[2,256,1024]{2,1,0:T(8,128)} %param.7, s32[]{:T(128)S(6)} %add.53, s32[]{:T(128)S(6)} %add.54), kind=kLoop, calls=%fused_computation.142 | loop fusion | bytes 524296 | tf_op jit(solution)/shard_map/dynamic_slice | solution.py:39
  10.1 3.9 %collective-permute-start.2 = (f32[32,1024]{1,0:T(8,128)}, f32[32,1024]{1,0:T(8,128)}, u32[]{:S(2)}, u32[]{:S(2)}) collective-permute-start(f32[32,1024]{1,0:T(8,128)} %get-tuple-element.8), channel_id=1, source_target_pairs={{0,3},{1,2},{2,1},{3,0},{4,7},{5,6},{6,5},{7,4},{8,11},{9,10},{10,... | collective-permute-start | bytes 393224 | tf_op jit(solution)/shard_map/ppermute | solution.py:13
  14.0 1.3 fusion.68
  15.3 2.0 %collective-permute-done = f32[32,1024]{1,0:T(8,128)S(1)} collective-permute-done((f32[32,1024]{1,0:T(8,128)}, f32[32,1024]{1,0:T(8,128)S(1)}, u32[]{:S(2)}, u32[]{:S(2)}) %collective-permute-start) | collective-permute-done | bytes 131104 | tf_op jit(solution)/shard_map/ppermute | solution.py:13
  17.3 2.7 %collective-permute-start.19 = (f32[128,256]{1,0:T(8,128)}, f32[128,256]{1,0:T(8,128)S(1)}, u32[]{:S(2)}, u32[]{:S(2)}) collective-permute-start(f32[128,256]{1,0:T(8,128)} %constant_dynamic-slice_fusion.1), channel_id=1, source_target_pairs={{0,3},{1,2},{2,1},{3,0},{4,7},{5,6},{6,5},{7,4},{8,11},{9,10},{10,... | collective-permute-start | bytes 393224 | tf_op jit(solution)/shard_map/ppermute | solution.py:13
  21.0 1.1 copy.29
  22.1 4.2 %collective-permute-done.1 = f32[32,1024]{1,0:T(8,128)S(1)} collective-permute-done((f32[32,1024]{1,0:T(8,128)}, f32[32,1024]{1,0:T(8,128)S(1)}, u32[]{:S(2)}, u32[]{:S(2)}) %collective-permute-start.1) | collective-permute-done | bytes 131104 | tf_op jit(solution)/shard_map/ppermute | solution.py:13
  26.5 4.7 %collective-permute-start.29 = (f32[64,2,256]{2,1,0:T(2,128)}, f32[64,2,256]{2,1,0:T(2,128)S(1)}, u32[]{:S(2)}, u32[]{:S(2)}) collective-permute-start(f32[64,2,256]{2,1,0:T(2,128)} %constant_dynamic-slice_fusion), channel_id=1, source_target_pairs={{0,2},{1,3},{2,0},{3,1},{4,6},{5,7},{6,4},{7,5},{8,10},{9,11},{10,... | collective-permute-start | bytes 393224 | tf_op jit(solution)/shard_map/ppermute | solution.py:13
  33.1 1.6 %collective-permute-start.3 = (f32[3,32,1024]{2,1,0:T(8,128)S(1)}, f32[3,32,1024]{2,1,0:T(8,128)S(1)}, u32[]{:S(2)}, u32[]{:S(2)}) collective-permute-start(f32[3,32,1024]{2,1,0:T(8,128)S(1)} %pad_maximum_fusion.18), channel_id=1, source_target_pairs={{0,4},{4,0},{8,12},{12,8},{1,5},{5,1},{9,13},{13,9},{2,6},{6,2},{1... | collective-permute-start | bytes 1179656 | tf_op jit(solution)/shard_map/ppermute | solution.py:13
  35.7 5.1 %collective-permute-done.29 = f32[64,2,256]{2,1,0:T(2,128)S(1)} collective-permute-done((f32[64,2,256]{2,1,0:T(2,128)}, f32[64,2,256]{2,1,0:T(2,128)S(1)}, u32[]{:S(2)}, u32[]{:S(2)}) %collective-permute-start.29) | collective-permute-done | bytes 131104 | tf_op jit(solution)/shard_map/ppermute | solution.py:13
  40.7 2.6 %collective-permute-start.12 = (f32[32,1024]{1,0:T(8,128)}, f32[32,1024]{1,0:T(8,128)S(1)}, u32[]{:S(2)}, u32[]{:S(2)}) collective-permute-start(f32[32,1024]{1,0:T(8,128)} %get-tuple-element.9), channel_id=1, source_target_pairs={{0,3},{1,2},{2,1},{3,0},{4,7},{5,6},{6,5},{7,4},{8,11},{9,10},{10,... | collective-permute-start | bytes 393224 | tf_op jit(solution)/shard_map/ppermute | solution.py:13
  43.6 1.6 %collective-permute-start.5 = (f32[3,32,1024]{2,1,0:T(8,128)S(1)}, f32[3,32,1024]{2,1,0:T(8,128)S(1)}, u32[]{:S(2)}, u32[]{:S(2)}) collective-permute-start(f32[3,32,1024]{2,1,0:T(8,128)S(1)} %pad_maximum_fusion.18), channel_id=1, source_target_pairs={{0,8},{4,12},{8,0},{12,4},{1,9},{5,13},{9,1},{13,5},{2,10},{6,14},... | collective-permute-start | bytes 1179656 | tf_op jit(solution)/shard_map/ppermute | solution.py:13
  45.2 6.8 %collective-permute-done.11 = f32[32,1024]{1,0:T(8,128)S(1)} collective-permute-done((f32[32,1024]{1,0:T(8,128)}, f32[32,1024]{1,0:T(8,128)S(1)}, u32[]{:S(2)}, u32[]{:S(2)}) %collective-permute-start.11) | collective-permute-done | bytes 131104 | tf_op jit(solution)/shard_map/ppermute | solution.py:13
  52.0 1.5 %collective-permute-start.20 = (f32[3,128,256]{2,1,0:T(8,128)S(1)}, f32[3,128,256]{2,1,0:T(8,128)S(1)}, u32[]{:S(2)}, u32[]{:S(2)}) collective-permute-start(f32[3,128,256]{2,1,0:T(8,128)S(1)} %pad_maximum_fusion.20), channel_id=1, source_target_pairs={{0,8},{4,12},{8,0},{12,4},{1,9},{5,13},{9,1},{13,5},{2,10},{6,14},... | collective-permute-start | bytes 1179656 | tf_op jit(solution)/shard_map/ppermute | solution.py:13
  54.0 1.5 %collective-permute-start.4 = (f32[3,32,1024]{2,1,0:T(8,128)S(1)}, f32[3,32,1024]{2,1,0:T(8,128)S(1)}, u32[]{:S(2)}, u32[]{:S(2)}) collective-permute-start(f32[3,32,1024]{2,1,0:T(8,128)S(1)} %collective-permute-done.3), channel_id=1, source_target_pairs={{0,8},{4,12},{8,0},{12,4},{1,9},{5,13},{9,1},{13,5},{2,10},{6,14},... | collective-permute-start | bytes 1179656 | tf_op jit(solution)/shard_map/ppermute | solution.py:13
  55.6 1.6 %collective-permute-start.22 = (f32[3,128,256]{2,1,0:T(8,128)S(1)}, f32[3,128,256]{2,1,0:T(8,128)S(1)}, u32[]{:S(2)}, u32[]{:S(2)}) collective-permute-start(f32[3,128,256]{2,1,0:T(8,128)S(1)} %pad_maximum_fusion.20), channel_id=1, source_target_pairs={{0,4},{4,0},{8,12},{12,8},{1,5},{5,1},{9,13},{13,9},{2,6},{6,2},{1... | collective-permute-start | bytes 1179656 | tf_op jit(solution)/shard_map/ppermute | solution.py:13
  58.5 14.0 %collective-permute-done.31 = f32[3,64,2,256]{3,2,1,0:T(2,128)S(1)} collective-permute-done((f32[3,64,2,256]{3,2,1,0:T(2,128)S(1)}, f32[3,64,2,256]{3,2,1,0:T(2,128)S(1)}, u32[]{:S(2)}, u32[]{:S(2)}) %collective-permute-start.31) | collective-permute-done | bytes 393248 | tf_op jit(solution)/shard_map/ppermute | solution.py:13
  72.5 1.4 %collective-permute-start.13 = (f32[3,32,1024]{2,1,0:T(8,128)S(1)}, f32[3,32,1024]{2,1,0:T(8,128)S(1)}, u32[]{:S(2)}, u32[]{:S(2)}) collective-permute-start(f32[3,32,1024]{2,1,0:T(8,128)S(1)} %pad_maximum_fusion.19), channel_id=1, source_target_pairs={{0,4},{4,0},{8,12},{12,8},{1,5},{5,1},{9,13},{13,9},{2,6},{6,2},{1... | collective-permute-start | bytes 1179656 | tf_op jit(solution)/shard_map/ppermute | solution.py:13
  73.9 5.7 %collective-permute-done.4 = f32[3,32,1024]{2,1,0:T(8,128)S(1)} collective-permute-done((f32[3,32,1024]{2,1,0:T(8,128)S(1)}, f32[3,32,1024]{2,1,0:T(8,128)S(1)}, u32[]{:S(2)}, u32[]{:S(2)}) %collective-permute-start.4) | collective-permute-done | bytes 393248 | tf_op jit(solution)/shard_map/ppermute | solution.py:13
  83.4 1.6 %collective-permute-start.15 = (f32[3,32,1024]{2,1,0:T(8,128)S(1)}, f32[3,32,1024]{2,1,0:T(8,128)S(1)}, u32[]{:S(2)}, u32[]{:S(2)}) collective-permute-start(f32[3,32,1024]{2,1,0:T(8,128)S(1)} %pad_maximum_fusion.19), channel_id=1, source_target_pairs={{0,8},{4,12},{8,0},{12,4},{1,9},{5,13},{9,1},{13,5},{2,10},{6,14},... | collective-permute-start | bytes 1179656 | tf_op jit(solution)/shard_map/ppermute | solution.py:13
  85.0 1.4 %collective-permute-start.21 = (f32[3,128,256]{2,1,0:T(8,128)S(1)}, f32[3,128,256]{2,1,0:T(8,128)S(1)}, u32[]{:S(2)}, u32[]{:S(2)}) collective-permute-start(f32[3,128,256]{2,1,0:T(8,128)S(1)} %collective-permute-done.20), channel_id=1, source_target_pairs={{0,4},{4,0},{8,12},{12,8},{1,5},{5,1},{9,13},{13,9},{2,6},{6,2},{1... | collective-permute-start | bytes 1179656 | tf_op jit(solution)/shard_map/ppermute | solution.py:13
  87.0 4.6 %collective-permute-done.32 = f32[3,64,2,256]{3,2,1,0:T(2,128)S(1)} collective-permute-done((f32[3,64,2,256]{3,2,1,0:T(2,128)S(1)}, f32[3,64,2,256]{3,2,1,0:T(2,128)S(1)}, u32[]{:S(2)}, u32[]{:S(2)}) %collective-permute-start.32) | collective-permute-done | bytes 393248 | tf_op jit(solution)/shard_map/ppermute | solution.py:13
  94.1 7.0 %collective-permute-start.9 = (f32[128,256]{1,0:T(8,128)S(1)}, f32[128,256]{1,0:T(8,128)S(1)}, u32[]{:S(2)}, u32[]{:S(2)}) collective-permute-start(f32[128,256]{1,0:T(8,128)S(1)} %fusion.13), channel_id=1, source_target_pairs={{0,1},{1,0},{2,3},{3,2},{4,5},{5,4},{6,7},{7,6},{8,9},{9,8},{10,11... | collective-permute-start | bytes 393224 | tf_op jit(solution)/shard_map/ppermute | solution.py:13
  102.0 2.4 %collective-permute-start.7 = (f32[128,256]{1,0:T(8,128)S(1)}, f32[128,256]{1,0:T(8,128)S(1)}, u32[]{:S(2)}, u32[]{:S(2)}) collective-permute-start(f32[128,256]{1,0:T(8,128)S(1)} %fusion.15), channel_id=1, source_target_pairs={{0,3},{1,2},{2,1},{3,0},{4,7},{5,6},{6,5},{7,4},{8,11},{9,10},{10,... | collective-permute-start | bytes 393224 | tf_op jit(solution)/shard_map/ppermute | solution.py:13
  105.2 5.0 %collective-permute-done.8 = f32[128,256]{1,0:T(8,128)S(1)} collective-permute-done((f32[128,256]{1,0:T(8,128)S(1)}, f32[128,256]{1,0:T(8,128)S(1)}, u32[]{:S(2)}, u32[]{:S(2)}) %collective-permute-start.8) | collective-permute-done | bytes 131104 | tf_op jit(solution)/shard_map/ppermute | solution.py:13
  116.4 2.0 %collective-permute-start.26 = (f32[128,256]{1,0:T(8,128)S(1)}, f32[128,256]{1,0:T(8,128)S(1)}, u32[]{:S(2)}, u32[]{:S(2)}) collective-permute-start(f32[128,256]{1,0:T(8,128)S(1)} %fusion.6), channel_id=1, source_target_pairs={{0,1},{1,0},{2,3},{3,2},{4,5},{5,4},{6,7},{7,6},{8,9},{9,8},{10,11... | collective-permute-start | bytes 393224 | tf_op jit(solution)/shard_map/ppermute | solution.py:13
  118.7 2.2 %collective-permute-start.24 = (f32[128,256]{1,0:T(8,128)S(1)}, f32[128,256]{1,0:T(8,128)S(1)}, u32[]{:S(2)}, u32[]{:S(2)}) collective-permute-start(f32[128,256]{1,0:T(8,128)S(1)} %fusion.11), channel_id=1, source_target_pairs={{0,3},{1,2},{2,1},{3,0},{4,7},{5,6},{6,5},{7,4},{8,11},{9,10},{10,... | collective-permute-start | bytes 393224 | tf_op jit(solution)/shard_map/ppermute | solution.py:13
  121.7 2.1 %collective-permute-done.26 = f32[128,256]{1,0:T(8,128)S(1)} collective-permute-done((f32[128,256]{1,0:T(8,128)S(1)}, f32[128,256]{1,0:T(8,128)S(1)}, u32[]{:S(2)}, u32[]{:S(2)}) %collective-permute-start.26) | collective-permute-done | bytes 131104 | tf_op jit(solution)/shard_map/ppermute | solution.py:13
  123.8 7.6 %collective-permute-done.25 = f32[128,256]{1,0:T(8,128)S(1)} collective-permute-done((f32[128,256]{1,0:T(8,128)S(1)}, f32[128,256]{1,0:T(8,128)S(1)}, u32[]{:S(2)}, u32[]{:S(2)}) %collective-permute-start.25) | collective-permute-done | bytes 131104 | tf_op jit(solution)/shard_map/ppermute | solution.py:13
  135.7 1.5 %pad_maximum_fusion = f32[2,256,1024]{2,1,0:T(8,128)} fusion(f32[2,128,1024]{2,1,0:T(8,128)S(1)} %get-tuple-element.7, f32[2,128,1024]{2,1,0:T(8,128)S(1)} %get-tuple-element.6), kind=kLoop, calls=%fused_computation | loop fusion | flops 524288 | bytes 4194304 | tf_op jit(solution)/shard_map/concatenate | solution.py:32
  (101 shorter events, 28.2 us)
Async XLA Ops:
  2.3 29.8 %collective-permute-start.17 = (f32[128,256]{1,0:T(8,128)}, f32[128,256]{1,0:T(8,128)S(1)}, u32[]{:S(2)}, u32[]{:S(2)}) collective-permute-start(f32[128,256]{1,0:T(8,128)} %constant_dynamic-slice_fusion.1), channel_id=1, source_target_pairs={{0,1},{1,0},{2,3},{3,2},{4,5},{5,4},{6,7},{7,6},{8,9},{9,8},{10,11... | collective-permute-start | bytes 393224 | tf_op jit(solution)/shard_map/ppermute | solution.py:13
  5.4 27.7 %collective-permute-start.18 = (f32[128,256]{1,0:T(8,128)}, f32[128,256]{1,0:T(8,128)S(1)}, u32[]{:S(2)}, u32[]{:S(2)}) collective-permute-start(f32[128,256]{1,0:T(8,128)} %constant_dynamic-slice_fusion.1), channel_id=1, source_target_pairs={{0,2},{1,3},{2,0},{3,1},{4,6},{5,7},{6,4},{7,5},{8,10},{9,11},{10,... | collective-permute-start | bytes 393224 | tf_op jit(solution)/shard_map/ppermute | solution.py:13
  9.7 7.6 %collective-permute-start = (f32[32,1024]{1,0:T(8,128)}, f32[32,1024]{1,0:T(8,128)S(1)}, u32[]{:S(2)}, u32[]{:S(2)}) collective-permute-start(f32[32,1024]{1,0:T(8,128)} %get-tuple-element.8), channel_id=1, source_target_pairs={{0,1},{1,0},{2,3},{3,2},{4,5},{5,4},{6,7},{7,6},{8,9},{9,8},{10,11... | collective-permute-start | bytes 393224 | tf_op jit(solution)/shard_map/ppermute | solution.py:13
  10.1 16.2 %collective-permute-start.1 = (f32[32,1024]{1,0:T(8,128)}, f32[32,1024]{1,0:T(8,128)S(1)}, u32[]{:S(2)}, u32[]{:S(2)}) collective-permute-start(f32[32,1024]{1,0:T(8,128)} %get-tuple-element.8), channel_id=1, source_target_pairs={{0,2},{1,3},{2,0},{3,1},{4,6},{5,7},{6,4},{7,5},{8,10},{9,11},{10,... | collective-permute-start | bytes 393224 | tf_op jit(solution)/shard_map/ppermute | solution.py:13
  10.1 16.4 %collective-permute-start.2 = (f32[32,1024]{1,0:T(8,128)}, f32[32,1024]{1,0:T(8,128)}, u32[]{:S(2)}, u32[]{:S(2)}) collective-permute-start(f32[32,1024]{1,0:T(8,128)} %get-tuple-element.8), channel_id=1, source_target_pairs={{0,3},{1,2},{2,1},{3,0},{4,7},{5,6},{6,5},{7,4},{8,11},{9,10},{10,... | collective-permute-start | bytes 393224 | tf_op jit(solution)/shard_map/ppermute | solution.py:13
  17.3 15.8 %collective-permute-start.19 = (f32[128,256]{1,0:T(8,128)}, f32[128,256]{1,0:T(8,128)S(1)}, u32[]{:S(2)}, u32[]{:S(2)}) collective-permute-start(f32[128,256]{1,0:T(8,128)} %constant_dynamic-slice_fusion.1), channel_id=1, source_target_pairs={{0,3},{1,2},{2,1},{3,0},{4,7},{5,6},{6,5},{7,4},{8,11},{9,10},{10,... | collective-permute-start | bytes 393224 | tf_op jit(solution)/shard_map/ppermute | solution.py:13
  26.3 8.8 %collective-permute-start.28 = (f32[64,2,256]{2,1,0:T(2,128)}, f32[64,2,256]{2,1,0:T(2,128)S(1)}, u32[]{:S(2)}, u32[]{:S(2)}) collective-permute-start(f32[64,2,256]{2,1,0:T(2,128)} %constant_dynamic-slice_fusion), channel_id=1, source_target_pairs={{0,1},{1,0},{2,3},{3,2},{4,5},{5,4},{6,7},{7,6},{8,9},{9,8},{10,11... | collective-permute-start | bytes 393224 | tf_op jit(solution)/shard_map/ppermute | solution.py:13
  26.5 14.2 %collective-permute-start.29 = (f32[64,2,256]{2,1,0:T(2,128)}, f32[64,2,256]{2,1,0:T(2,128)S(1)}, u32[]{:S(2)}, u32[]{:S(2)}) collective-permute-start(f32[64,2,256]{2,1,0:T(2,128)} %constant_dynamic-slice_fusion), channel_id=1, source_target_pairs={{0,2},{1,3},{2,0},{3,1},{4,6},{5,7},{6,4},{7,5},{8,10},{9,11},{10,... | collective-permute-start | bytes 393224 | tf_op jit(solution)/shard_map/ppermute | solution.py:13
  32.2 8.6 %collective-permute-start.30 = (f32[64,2,256]{2,1,0:T(2,128)}, f32[64,2,256]{2,1,0:T(2,128)S(1)}, u32[]{:S(2)}, u32[]{:S(2)}) collective-permute-start(f32[64,2,256]{2,1,0:T(2,128)} %constant_dynamic-slice_fusion), channel_id=1, source_target_pairs={{0,3},{1,2},{2,1},{3,0},{4,7},{5,6},{6,5},{7,4},{8,11},{9,10},{10,... | collective-permute-start | bytes 393224 | tf_op jit(solution)/shard_map/ppermute | solution.py:13
  33.1 22.4 %collective-permute-start.6 = (f32[512,256]{0,1:T(8,128)S(1)}, f32[512,256]{0,1:T(8,128)S(1)}, u32[]{:S(2)}, u32[]{:S(2)}) collective-permute-start(f32[512,256]{0,1:T(8,128)S(1)} %bitcast.139), channel_id=1, source_target_pairs={{0,16},{16,0},{1,17},{17,1},{2,18},{18,2},{3,19},{19,3},{4,20},{20... | collective-permute-start | bytes 1572872 | tf_op jit(solution)/shard_map/ppermute | solution.py:13
  33.1 20.9 %collective-permute-start.3 = (f32[3,32,1024]{2,1,0:T(8,128)S(1)}, f32[3,32,1024]{2,1,0:T(8,128)S(1)}, u32[]{:S(2)}, u32[]{:S(2)}) collective-permute-start(f32[3,32,1024]{2,1,0:T(8,128)S(1)} %pad_maximum_fusion.18), channel_id=1, source_target_pairs={{0,4},{4,0},{8,12},{12,8},{1,5},{5,1},{9,13},{13,9},{2,6},{6,2},{1... | collective-permute-start | bytes 1179656 | tf_op jit(solution)/shard_map/ppermute | solution.py:13
  35.1 8.5 %collective-permute-start.10 = (f32[32,1024]{1,0:T(8,128)}, f32[32,1024]{1,0:T(8,128)S(1)}, u32[]{:S(2)}, u32[]{:S(2)}) collective-permute-start(f32[32,1024]{1,0:T(8,128)} %get-tuple-element.9), channel_id=1, source_target_pairs={{0,1},{1,0},{2,3},{3,2},{4,5},{5,4},{6,7},{7,6},{8,9},{9,8},{10,11... | collective-permute-start | bytes 393224 | tf_op jit(solution)/shard_map/ppermute | solution.py:13
  40.7 11.2 %collective-permute-start.11 = (f32[32,1024]{1,0:T(8,128)}, f32[32,1024]{1,0:T(8,128)S(1)}, u32[]{:S(2)}, u32[]{:S(2)}) collective-permute-start(f32[32,1024]{1,0:T(8,128)} %get-tuple-element.9), channel_id=1, source_target_pairs={{0,2},{1,3},{2,0},{3,1},{4,6},{5,7},{6,4},{7,5},{8,10},{9,11},{10,... | collective-permute-start | bytes 393224 | tf_op jit(solution)/shard_map/ppermute | solution.py:13
  40.7 12.8 %collective-permute-start.12 = (f32[32,1024]{1,0:T(8,128)}, f32[32,1024]{1,0:T(8,128)S(1)}, u32[]{:S(2)}, u32[]{:S(2)}) collective-permute-start(f32[32,1024]{1,0:T(8,128)} %get-tuple-element.9), channel_id=1, source_target_pairs={{0,3},{1,2},{2,1},{3,0},{4,7},{5,6},{6,5},{7,4},{8,11},{9,10},{10,... | collective-permute-start | bytes 393224 | tf_op jit(solution)/shard_map/ppermute | solution.py:13
  43.6 14.3 %collective-permute-start.5 = (f32[3,32,1024]{2,1,0:T(8,128)S(1)}, f32[3,32,1024]{2,1,0:T(8,128)S(1)}, u32[]{:S(2)}, u32[]{:S(2)}) collective-permute-start(f32[3,32,1024]{2,1,0:T(8,128)S(1)} %pad_maximum_fusion.18), channel_id=1, source_target_pairs={{0,8},{4,12},{8,0},{12,4},{1,9},{5,13},{9,1},{13,5},{2,10},{6,14},... | collective-permute-start | bytes 1179656 | tf_op jit(solution)/shard_map/ppermute | solution.py:13
  52.0 31.4 %collective-permute-start.20 = (f32[3,128,256]{2,1,0:T(8,128)S(1)}, f32[3,128,256]{2,1,0:T(8,128)S(1)}, u32[]{:S(2)}, u32[]{:S(2)}) collective-permute-start(f32[3,128,256]{2,1,0:T(8,128)S(1)} %pad_maximum_fusion.20), channel_id=1, source_target_pairs={{0,8},{4,12},{8,0},{12,4},{1,9},{5,13},{9,1},{13,5},{2,10},{6,14},... | collective-permute-start | bytes 1179656 | tf_op jit(solution)/shard_map/ppermute | solution.py:13
  53.5 19.0 %collective-permute-start.31 = (f32[3,64,2,256]{3,2,1,0:T(2,128)S(1)}, f32[3,64,2,256]{3,2,1,0:T(2,128)S(1)}, u32[]{:S(2)}, u32[]{:S(2)}) collective-permute-start(f32[3,64,2,256]{3,2,1,0:T(2,128)S(1)} %pad_maximum_fusion.21), channel_id=1, source_target_pairs={{0,8},{4,12},{8,0},{12,4},{1,9},{5,13},{9,1},{13,5},{2,10},{6,14},... | collective-permute-start | bytes 1179656 | tf_op jit(solution)/shard_map/ppermute | solution.py:13
  54.0 25.6 %collective-permute-start.4 = (f32[3,32,1024]{2,1,0:T(8,128)S(1)}, f32[3,32,1024]{2,1,0:T(8,128)S(1)}, u32[]{:S(2)}, u32[]{:S(2)}) collective-permute-start(f32[3,32,1024]{2,1,0:T(8,128)S(1)} %collective-permute-done.3), channel_id=1, source_target_pairs={{0,8},{4,12},{8,0},{12,4},{1,9},{5,13},{9,1},{13,5},{2,10},{6,14},... | collective-permute-start | bytes 1179656 | tf_op jit(solution)/shard_map/ppermute | solution.py:13
  55.6 46.4 %collective-permute-start.22 = (f32[3,128,256]{2,1,0:T(8,128)S(1)}, f32[3,128,256]{2,1,0:T(8,128)S(1)}, u32[]{:S(2)}, u32[]{:S(2)}) collective-permute-start(f32[3,128,256]{2,1,0:T(8,128)S(1)} %pad_maximum_fusion.20), channel_id=1, source_target_pairs={{0,4},{4,0},{8,12},{12,8},{1,5},{5,1},{9,13},{13,9},{2,6},{6,2},{1... | collective-permute-start | bytes 1179656 | tf_op jit(solution)/shard_map/ppermute | solution.py:13
  57.9 28.5 %collective-permute-start.33 = (f32[3,64,2,256]{3,2,1,0:T(2,128)S(1)}, f32[3,64,2,256]{3,2,1,0:T(2,128)S(1)}, u32[]{:S(2)}, u32[]{:S(2)}) collective-permute-start(f32[3,64,2,256]{3,2,1,0:T(2,128)S(1)} %pad_maximum_fusion.21), channel_id=1, source_target_pairs={{0,4},{4,0},{8,12},{12,8},{1,5},{5,1},{9,13},{13,9},{2,6},{6,2},{1... | collective-permute-start | bytes 1179656 | tf_op jit(solution)/shard_map/ppermute | solution.py:13
  72.5 12.5 %collective-permute-start.13 = (f32[3,32,1024]{2,1,0:T(8,128)S(1)}, f32[3,32,1024]{2,1,0:T(8,128)S(1)}, u32[]{:S(2)}, u32[]{:S(2)}) collective-permute-start(f32[3,32,1024]{2,1,0:T(8,128)S(1)} %pad_maximum_fusion.19), channel_id=1, source_target_pairs={{0,4},{4,0},{8,12},{12,8},{1,5},{5,1},{9,13},{13,9},{2,6},{6,2},{1... | collective-permute-start | bytes 1179656 | tf_op jit(solution)/shard_map/ppermute | solution.py:13
  79.6 12.0 %collective-permute-start.32 = (f32[3,64,2,256]{3,2,1,0:T(2,128)S(1)}, f32[3,64,2,256]{3,2,1,0:T(2,128)S(1)}, u32[]{:S(2)}, u32[]{:S(2)}) collective-permute-start(f32[3,64,2,256]{3,2,1,0:T(2,128)S(1)} %collective-permute-done.31), channel_id=1, source_target_pairs={{0,4},{4,0},{8,12},{12,8},{1,5},{5,1},{9,13},{13,9},{2,6},{6,2},{1... | collective-permute-start | bytes 1179656 | tf_op jit(solution)/shard_map/ppermute | solution.py:13
  83.4 21.2 %collective-permute-start.15 = (f32[3,32,1024]{2,1,0:T(8,128)S(1)}, f32[3,32,1024]{2,1,0:T(8,128)S(1)}, u32[]{:S(2)}, u32[]{:S(2)}) collective-permute-start(f32[3,32,1024]{2,1,0:T(8,128)S(1)} %pad_maximum_fusion.19), channel_id=1, source_target_pairs={{0,8},{4,12},{8,0},{12,4},{1,9},{5,13},{9,1},{13,5},{2,10},{6,14},... | collective-permute-start | bytes 1179656 | tf_op jit(solution)/shard_map/ppermute | solution.py:13
  85.0 17.0 %collective-permute-start.21 = (f32[3,128,256]{2,1,0:T(8,128)S(1)}, f32[3,128,256]{2,1,0:T(8,128)S(1)}, u32[]{:S(2)}, u32[]{:S(2)}) collective-permute-start(f32[3,128,256]{2,1,0:T(8,128)S(1)} %collective-permute-done.20), channel_id=1, source_target_pairs={{0,4},{4,0},{8,12},{12,8},{1,5},{5,1},{9,13},{13,9},{2,6},{6,2},{1... | collective-permute-start | bytes 1179656 | tf_op jit(solution)/shard_map/ppermute | solution.py:13
  86.5 18.2 %collective-permute-start.14 = (f32[3,32,1024]{2,1,0:T(8,128)S(1)}, f32[3,32,1024]{2,1,0:T(8,128)S(1)}, u32[]{:S(2)}, u32[]{:S(2)}) collective-permute-start(f32[3,32,1024]{2,1,0:T(8,128)S(1)} %collective-permute-done.13), channel_id=1, source_target_pairs={{0,8},{4,12},{8,0},{12,4},{1,9},{5,13},{9,1},{13,5},{2,10},{6,14},... | collective-permute-start | bytes 1179656 | tf_op jit(solution)/shard_map/ppermute | solution.py:13
  94.1 11.1 %collective-permute-start.9 = (f32[128,256]{1,0:T(8,128)S(1)}, f32[128,256]{1,0:T(8,128)S(1)}, u32[]{:S(2)}, u32[]{:S(2)}) collective-permute-start(f32[128,256]{1,0:T(8,128)S(1)} %fusion.13), channel_id=1, source_target_pairs={{0,1},{1,0},{2,3},{3,2},{4,5},{5,4},{6,7},{7,6},{8,9},{9,8},{10,11... | collective-permute-start | bytes 393224 | tf_op jit(solution)/shard_map/ppermute | solution.py:13
  102.0 8.2 %collective-permute-start.8 = (f32[128,256]{1,0:T(8,128)S(1)}, f32[128,256]{1,0:T(8,128)S(1)}, u32[]{:S(2)}, u32[]{:S(2)}) collective-permute-start(f32[128,256]{1,0:T(8,128)S(1)} %fusion.14), channel_id=1, source_target_pairs={{0,2},{1,3},{2,0},{3,1},{4,6},{5,7},{6,4},{7,5},{8,10},{9,11},{10,... | collective-permute-start | bytes 393224 | tf_op jit(solution)/shard_map/ppermute | solution.py:13
  102.0 8.1 %collective-permute-start.7 = (f32[128,256]{1,0:T(8,128)S(1)}, f32[128,256]{1,0:T(8,128)S(1)}, u32[]{:S(2)}, u32[]{:S(2)}) collective-permute-start(f32[128,256]{1,0:T(8,128)S(1)} %fusion.15), channel_id=1, source_target_pairs={{0,3},{1,2},{2,1},{3,0},{4,7},{5,6},{6,5},{7,4},{8,11},{9,10},{10,... | collective-permute-start | bytes 393224 | tf_op jit(solution)/shard_map/ppermute | solution.py:13
  116.4 7.3 %collective-permute-start.26 = (f32[128,256]{1,0:T(8,128)S(1)}, f32[128,256]{1,0:T(8,128)S(1)}, u32[]{:S(2)}, u32[]{:S(2)}) collective-permute-start(f32[128,256]{1,0:T(8,128)S(1)} %fusion.6), channel_id=1, source_target_pairs={{0,1},{1,0},{2,3},{3,2},{4,5},{5,4},{6,7},{7,6},{8,9},{9,8},{10,11... | collective-permute-start | bytes 393224 | tf_op jit(solution)/shard_map/ppermute | solution.py:13
  118.5 12.9 %collective-permute-start.25 = (f32[128,256]{1,0:T(8,128)S(1)}, f32[128,256]{1,0:T(8,128)S(1)}, u32[]{:S(2)}, u32[]{:S(2)}) collective-permute-start(f32[128,256]{1,0:T(8,128)S(1)} %fusion.7), channel_id=1, source_target_pairs={{0,2},{1,3},{2,0},{3,1},{4,6},{5,7},{6,4},{7,5},{8,10},{9,11},{10,... | collective-permute-start | bytes 393224 | tf_op jit(solution)/shard_map/ppermute | solution.py:13
  118.7 12.7 %collective-permute-start.24 = (f32[128,256]{1,0:T(8,128)S(1)}, f32[128,256]{1,0:T(8,128)S(1)}, u32[]{:S(2)}, u32[]{:S(2)}) collective-permute-start(f32[128,256]{1,0:T(8,128)S(1)} %fusion.11), channel_id=1, source_target_pairs={{0,3},{1,2},{2,1},{3,0},{4,7},{5,6},{6,5},{7,4},{8,11},{9,10},{10,... | collective-permute-start | bytes 393224 | tf_op jit(solution)/shard_map/ppermute | solution.py:13
  121.6 11.0 %collective-permute-start.34 = (f32[4,128,256]{2,1,0:T(8,128)S(1)}, f32[4,128,256]{2,1,0:T(8,128)S(1)}, u32[]{:S(2)}, u32[]{:S(2)}) collective-permute-start(f32[4,128,256]{2,1,0:T(8,128)S(1)} %pad_maximum_fusion.9), channel_id=1, source_target_pairs={{0,16},{16,0},{1,17},{17,1},{2,18},{18,2},{3,19},{19,3},{4,20},{20... | collective-permute-start | bytes 1572872 | tf_op jit(solution)/shard_map/ppermute | solution.py:13
  (6 other events, 44.5 us)
where the time goes:
time: 137 us
  waiting for transfers between devices  57.5 us (42%)
  starting transfers between devices  50.2 us (37%)
  matrix products  10.5 us (8%)
  local copies, waits for them, and re-layouts  9.77 us (7%)
  other arithmetic  7.91 us (6%)
    ppermute x35, waiting for transfers between devices, exchange(): return lax.ppermute(value, axis, [(i, i ^ flip) for i in range(size)])  57.5 us
    ppermute x35, starting transfers between devices, exchange(): return lax.ppermute(value, axis, [(i, i ^ flip) for i in range(size)])  50.2 us
    dot_general x20, matrix products, product(): jnp.dot(left, right, precision=lax.Precision.HIGH, preferred_element_type...  10.5 us
    unnamed x10, local copies, waits for them, and re-layouts  3.34 us
    dynamic_slice x3, local copies, waits for them, and re-layouts, own_part(): lax.dynamic_slice_in_dim(value, lax.axis_index(axis) * size, size, dim)  3 us
  transfers between devices with their start and end apart: 35, of which 12 were waited for; matrix products, arithmetic and copies ran while one was open for 15% of the time, Pallas kernels for 0%

commit v1 on v0

v1 whole, which is shorter than its diff:
```python
import functools

import jax
import jax.numpy as jnp
from jax import lax
from jax.experimental import pallas as pl
from jax.experimental.pallas import tpu as pltpu
from jax.sharding import PartitionSpec as P


def exchange(value, axis, flip):
    pairs = [(i, i ^ flip) for i in range(lax.axis_size(axis))]
    return lax.ppermute(value, axis, pairs)


def in_order(blocks, index):
    bit = 1
    while bit < len(blocks):
        odd = (index & bit) != 0
        blocks = [jnp.where(odd, blocks[k ^ bit], blocks[k]) for k in range(len(blocks))]
        bit *= 2
    return blocks


def share_rows(value, dim):
    index = lax.axis_index("row")
    bit = 1
    while bit < lax.axis_size("row"):
        other = exchange(value, "row", bit)
        odd = (index & bit) != 0
        value = jnp.concatenate([jnp.where(odd, other, value), jnp.where(odd, value, other)], axis=dim)
        bit *= 2
    return value


def own_part(value, dim, axis):
    size = value.shape[dim] // lax.axis_size(axis)
    return lax.dynamic_slice_in_dim(value, lax.axis_index(axis) * size, size, dim)


def from_depth(part, relay):
    size = lax.axis_size("depth")
    if not (relay and size == 4):
        return jnp.stack([exchange(part, "depth", k) for k in range(1, size)])
    near = exchange(part, "depth", 1)
    across = lax.ppermute(jnp.stack([part, near]), "depth", [(1, 2), (2, 1)])
    handed = lax.ppermute(across, "depth", [(1, 0), (2, 3)])
    index = lax.axis_index("depth")
    outer = (index == 0) | (index == size - 1)
    far = [jnp.where(outer, handed[0], across[1]), jnp.where(outer, handed[1], across[0])]
    return jnp.stack([near] + far)


def from_columns(parts, low_first):
    size = lax.axis_size("col")
    bits = [1 << b for b in range(size.bit_length() - 1)]
    known = {0: parts}
    for bit in bits:
        known[bit] = exchange(parts, "col", bit)
    for k in range(1, size):
        if k not in known:
            via = [b for b in (bits if low_first else bits[::-1]) if k & b][-1]
            known[k] = exchange(known[k ^ via], "col", via)
    return [known[k] for k in range(size)]


def gather_factor(own, low_first, relay):
    return from_columns(from_depth(own_part(own, 0, "col"), relay), low_first)


def halves(value):
    high = value.astype(jnp.bfloat16)
    return high, (value - high.astype(jnp.float32)).astype(jnp.bfloat16)


def product(left, right):
    left_high, left_low = halves(left)
    right_high, right_low = right
    dot = functools.partial(jnp.dot, preferred_element_type=jnp.float32)
    return dot(left_high, right_high) + (dot(left_high, right_low) + dot(left_low, right_high))


def solve_kernel(place, own, *rest):
    *parts, rhs, out = rest
    right = halves(rhs[...])
    count, size, depth = parts[0].shape
    out[0] = product(own[0], right)
    left = jnp.concatenate([part[...].reshape(count * size, depth) for part in parts])
    rows = product(left, right)
    for k in range(len(parts)):
        at = pl.multiple_of((place[1] ^ k) * size, size)
        for j in range(count):
            from_row = (k * count + j) * size
            out[j + 1, pl.ds(at, size), :] = rows[from_row : from_row + size]


def update_kernel(quarters, place, own, *rest):
    *solved, base, out = rest[quarters:]
    parts = rest[:quarters]
    count, size, _ = parts[0].shape
    depth = solved[0].shape[1]
    near = far = None
    for s, blocks in enumerate(solved):
        at = slice(s * depth, (s + 1) * depth)
        for j in range(count + 1):
            right = halves(blocks[j])
            if j == 0:
                term = product(own[:, at], right)
                near = term if near is None else near + term
            else:
                left = jnp.concatenate([part[j - 1][:, at] for part in parts])
                term = product(left, right)
                far = term if far is None else far + term
    out[...] = base[...] - near
    for k in range(quarters):
        at = pl.ds(pl.multiple_of((place[1] ^ k) * size, size), size)
        out[at, :] = out[at, :] - far[k * size : (k + 1) * size]


def whole(array):
    zeros = (0,) * array.ndim
    return pl.BlockSpec(array.shape, lambda i, p: zeros)


def cost(flops, arrays):
    moved = sum(4 * a.size for a in arrays)
    return pl.CostEstimate(flops=flops, bytes_accessed=moved, transcendentals=0)


def call_kernel(kernel, place, first_spec, operands, shape, flops):
    out = jax.ShapeDtypeStruct(shape, jnp.float32)
    return pl.pallas_call(
        kernel,
        out_shape=out,
        grid_spec=pltpu.PrefetchScalarGridSpec(
            num_scalar_prefetch=1,
            grid=(1,),
            in_specs=[first_spec] + [whole(a) for a in operands[1:]],
            out_specs=whole(out),
        ),
        cost_estimate=cost(flops, operands[1:]),
    )(place, *operands)


def plain_product(left, right):
    return jnp.dot(left, right, precision=lax.Precision.HIGH, preferred_element_type=jnp.float32)


def solve(place, section, inverses, parts, rhs):
    rows = inverses.shape[1] // lax.axis_size("row")
    nb, cols = rhs.shape
    count, size, _ = parts[0].shape
    if size % 8:
        own = plain_product(own_part(inverses[section], 0, "row"), rhs)
        ordered = jnp.concatenate(in_order(list(parts), place[1]), axis=1)
        return jnp.stack([own] + [plain_product(ordered[j], rhs) for j in range(count)])
    spec = pl.BlockSpec((1, rows, nb), lambda i, p: (section, p[0], 0))
    shape = (count + 1, rows, cols)
    flops = 6 * (count + 1) * rows * nb * cols
    return call_kernel(solve_kernel, place, spec, (inverses, *parts, rhs), shape, flops)


def update(place, own, parts, solved, base):
    count, size, _ = parts[0].shape
    depth = solved[0].shape[1]
    if size % 8:
        ordered = jnp.concatenate(in_order(list(parts), place[1]), axis=1)
        for s, blocks in enumerate(solved):
            at = slice(s * depth, (s + 1) * depth)
            base = base - plain_product(own[:, at], blocks[0])
            for j in range(count):
                base = base - plain_product(ordered[j][:, at], blocks[j + 1])
        return base
    kernel = functools.partial(update_kernel, len(parts))
    flops = 6 * own.size * (count + 1) * base.shape[1]
    return call_kernel(kernel, place, whole(own), (own, *parts, *solved, base), base.shape, flops)


def to_output(parts):
    arrived = [parts[0]]
    for k in range(1, parts.shape[0]):
        arrived.append(exchange(parts[k], "depth", k))
    placed = jnp.concatenate(in_order(arrived, lax.axis_index("depth")), axis=1)
    return share_rows(placed, 0)


def steps(head_rhs, head_factor, inverses, trail_factor, trail_rhs):
    place = jnp.stack([lax.axis_index("row"), lax.axis_index("col")])
    lower = own_part(inverses, 1, "row")
    count = trail_factor.shape[0]
    trail_own = trail_factor.reshape(count, -1)
    trail_part = own_part(trail_factor, 0, "col").reshape(count // lax.axis_size("col"), -1)
    first_factor = gather_factor(lower[0], True, False)
    mid_factor = gather_factor(head_factor, False, True)
    second_factor = gather_factor(lower[1], True, True)
    trail_parts = from_columns(from_depth(trail_part, True), False)

    rhs = share_rows(head_rhs[0], 0)
    first_part = solve(place, 0, inverses, first_factor, rhs)
    first = share_rows(first_part, 1)
    second_rhs = update(place, head_factor, mid_factor, [first], head_rhs[1])
    second_rhs = share_rows(second_rhs, 0)
    second_part = solve(place, 1, inverses, second_factor, second_rhs)
    second = share_rows(second_part, 1)
    trail_out = update(place, trail_own, trail_parts, [first, second], trail_rhs)
    return jnp.stack([to_output(first_part), to_output(second_part)]), trail_out


def solution(mesh):
    placed = (
        P(None, "row", ("col", "depth")),
        P("row", "depth"),
        P(None, "depth", None),
        P("row", None, "depth"),
        P("row", ("col", "depth")),
    )
    return jax.shard_map(
        steps,
        mesh=mesh,
        in_specs=placed,
        out_specs=(P(None, "depth", "col"), P("row", ("col", "depth"))),
        check_vma=False,
    )
```

time: 137 us -> 156 us (1.14)
  Pallas kernels: 0 us -> 17.7 us
  matrix products: 10.5 us -> 0 us
  other arithmetic: 7.91 us -> 16.1 us
  starting transfers between devices: 50.2 us -> 54.9 us
  waiting for transfers between devices: 57.5 us -> 55.8 us
    pallas_call x0 -> x4, Pallas kernels: none -> 17.7 us  [call_kernel(): pl.pallas_call(kernel, out_shape=out, grid_spec=pltpu.PrefetchScalarGridS...]
    dot_general x20 -> x0, matrix products: 10.5 us -> none  [product(): jnp.dot(left, right, precision=lax.Precision.HIGH, preferred_element_type...]
    ppermute x35 -> x36, starting transfers between devices: 50.2 us -> 54.9 us  [the longest x30 46.9 us: exchange(): return lax.ppermute(value, axis, pairs)]
    squeeze x1 -> x3, local copies, waits for them, and re-layouts: 0.54 us -> 5.08 us  [the longest x2 2.84 us: to_output(): arrived.append(exchange(parts[k], 'depth', k))]
    select_n x1 -> x3, other arithmetic: 0.09 us -> 3.37 us  [from_depth(): jnp.where(outer, handed[0], across[1])]
    slice x4 -> x0, local copies, waits for them, and re-layouts: 2.89 us -> none  [the longest x3 1.62 us: steps(): trail[k][:, 1, :]]
    concatenate x1 -> x4, other arithmetic: 1.46 us -> 4.25 us  [share_rows(): jnp.concatenate([jnp.where(odd, other, value), jnp.where(odd, value, othe...]
    another operation x8 -> x10, other arithmetic: 2.41 us -> 4.91 us  [the longest x2 1.64 us: steps(): jnp.stack([to_output(first_part), to_output(second_part)])]
  transfers between devices with their start and end apart: 35 -> 36, of which waited for: 12 -> 9; matrix products, arithmetic and copies ran while one was open for 15% -> 13% of each run, Pallas kernels for 0% -> 11%
where the time goes in v1:
time: 156 us; the launch traced here: 155 us
  waiting for transfers between devices  55.8 us (36%)
  starting transfers between devices  54.9 us (35%)
  Pallas kernels  17.7 us (11%)
  other arithmetic  16.1 us (10%)
  local copies, waits for them, and re-layouts  9.97 us (6%)
    ppermute x30, starting transfers between devices, exchange(): return lax.ppermute(value, axis, pairs)  46.9 us
    ppermute x30, waiting for transfers between devices, exchange(): return lax.ppermute(value, axis, pairs)  45.3 us
    pallas_call x4, Pallas kernels, call_kernel(): pl.pallas_call(kernel, out_shape=out, grid_spec=pltpu.PrefetchScalarGridS...  17.7 us
    ppermute x3, waiting for transfers between devices, from_depth(): handed = lax.ppermute(across, 'depth', [(1, 0), (2, 3)])  10.5 us
    concatenate x4, other arithmetic, share_rows(): jnp.concatenate([jnp.where(odd, other, value), jnp.where(odd, value, othe...  4.25 us
    ppermute x3, starting transfers between devices, from_depth(): across = lax.ppermute(jnp.stack([part, near]), 'depth', [(1, 2), (2, 1)])  4.1 us
    ppermute x3, starting transfers between devices, from_depth(): handed = lax.ppermute(across, 'depth', [(1, 0), (2, 3)])  3.87 us
    select_n x3, other arithmetic, from_depth(): jnp.where(outer, handed[0], across[1])  3.37 us
  transfers between devices with their start and end apart: 36, of which 9 were waited for; matrix products, arithmetic and copies ran while one was open for 13% of the time, Pallas kernels for 11%

profile of v1, /device:TPU:0, one launch (start us, length us, event | category | flops | bytes accessed | tf_op | source)
XLA Modules:
  0.0 155.4 jit_solution(11416627735960711123)
XLA Ops:
  1.7 3.1 %collective-permute-start = (f32[32,1024]{1,0:T(8,128)S(1)}, f32[32,1024]{1,0:T(8,128)}, u32[]{:S(2)}, u32[]{:S(2)}) collective-permute-start(f32[32,1024]{1,0:T(8,128)S(1)} %get-tuple-element.2), channel_id=1, source_target_pairs={{0,1},{1,0},{2,3},{3,2},{4,5},{5,4},{6,7},{7,6},{8,9},{9,8},{10,11... | collective-permute-start | bytes 393224 | tf_op jit(solution)/shard_map/ppermute | solution.py:13
  4.9 2.6 %collective-permute-start.1 = (f32[32,1024]{1,0:T(8,128)S(1)}, f32[32,1024]{1,0:T(8,128)}, u32[]{:S(2)}, u32[]{:S(2)}) collective-permute-start(f32[32,1024]{1,0:T(8,128)S(1)} %get-tuple-element.2), channel_id=1, source_target_pairs={{0,2},{1,3},{2,0},{3,1},{4,6},{5,7},{6,4},{7,5},{8,10},{9,11},{10,... | collective-permute-start | bytes 393224 | tf_op jit(solution)/shard_map/ppermute | solution.py:13
  7.4 2.2 %slice_bitcast_fusion = (f32[512,256]{1,0:T(8,128)}, f32[512,256]{1,0:T(8,128)}) fusion(f32[2,512,256]{2,1,0:T(8,128)} %param.5), kind=kLoop, calls=%fused_computation.9 | loop fusion | bytes 2097152 | tf_op jit(solution)/shard_map/squeeze | solution.py:201
  12.6 5.2 %collective-permute-done.1 = f32[32,1024]{1,0:T(8,128)} collective-permute-done((f32[32,1024]{1,0:T(8,128)S(1)}, f32[32,1024]{1,0:T(8,128)}, u32[]{:S(2)}, u32[]{:S(2)}) %collective-permute-start.1) | collective-permute-done | bytes 131104 | tf_op jit(solution)/shard_map/ppermute | solution.py:13
  19.6 1.6 collective-permute-start.3
  21.2 1.4 collective-permute-start.18
  23.3 1.4 collective-permute-start.12
  25.7 1.4 collective-permute-start.30
  27.7 1.6 %collective-permute-start.4 = (f32[3,32,1024]{2,1,0:T(8,128)S(1)}, f32[3,32,1024]{2,1,0:T(8,128)S(1)}, u32[]{:S(2)}, u32[]{:S(2)}) collective-permute-start(f32[3,32,1024]{2,1,0:T(8,128)S(1)} %pad_maximum_fusion.7.rest_0_), channel_id=1, source_target_pairs={{0,8},{4,12},{8,0},{12,4},{1,9},{5,13},{9,1},{13,5},{2,10},{6,14},... | collective-permute-start | bytes 1179656 | tf_op jit(solution)/shard_map/ppermute | solution.py:13
  30.7 1.3 collective-permute-start.13
  34.9 10.5 %collective-permute-done.19 = f32[2,128,256]{2,1,0:T(8,128)S(1)} collective-permute-done((f32[2,128,256]{2,1,0:T(8,128)}, f32[2,128,256]{2,1,0:T(8,128)S(1)}, u32[]{:S(2)}, u32[]{:S(2)}) %collective-permute-start.19) | collective-permute-done | bytes 262176 | tf_op jit(solution)/shard_map/ppermute | solution.py:47
  46.4 1.6 %collective-permute-start.21 = (f32[3,128,256]{2,1,0:T(8,128)S(1)}, f32[3,128,256]{2,1,0:T(8,128)S(1)}, u32[]{:S(2)}, u32[]{:S(2)}) collective-permute-start(f32[3,128,256]{2,1,0:T(8,128)S(1)} %pad_maximum_fusion.9.rest_0_), channel_id=1, source_target_pairs={{0,8},{4,12},{8,0},{12,4},{1,9},{5,13},{9,1},{13,5},{2,10},{6,14},... | collective-permute-start | bytes 1179656 | tf_op jit(solution)/shard_map/ppermute | solution.py:13
  49.3 4.3 %shard_map.68 = f32[4,128,256]{2,1,0:T(8,128)} custom-call(s32[2]{0:T(128)} %pad_add_fusion.place, f32[2,256,1024]{2,1,0:T(8,128)} %own.5, f32[3,32,1024]{2,1,0:T(8,128)} %copy-done.6, f32[3,32,1024]{2,1,0:T(8,128)} %collective-permute-done.3.rest_1_, f32[3,32,1024]{2,1,0:T(8,128)} %copy-done.13, f32[3,32,1024]{2,1,0:T(8,128)} %collective-permute-done.5.rest_3_, ...), custom_call_target="tpu_custom_call" | custom-call | flops 805306368 | bytes 2621440 | tf_op jit(solution)/shard_map/pallas_call | solution.py:132
  54.9 1.6 collective-permute-start.14
  56.4 1.8 %slice_bitcast_fusion.7 = (f32[128,256]{1,0:T(8,128)}, f32[128,256]{1,0:T(8,128)}, f32[128,256]{1,0:T(8,128)}) fusion(f32[4,128,256]{2,1,0:T(8,128)} %shard_map.68), kind=kLoop, calls=%fused_computation.41 | loop fusion | bytes 786432 | tf_op jit(solution)/shard_map/squeeze | solution.py:182
  58.2 5.1 %collective-permute-start.7 = (f32[128,256]{1,0:T(8,128)}, f32[128,256]{1,0:T(8,128)S(1)}, u32[]{:S(2)}, u32[]{:S(2)}) collective-permute-start(f32[128,256]{1,0:T(8,128)} %get-tuple-element.30), channel_id=1, source_target_pairs={{0,3},{1,2},{2,1},{3,0},{4,7},{5,6},{6,5},{7,4},{8,11},{9,10},{10,... | collective-permute-start | bytes 393224 | tf_op jit(solution)/shard_map/ppermute | solution.py:13
  65.1 6.3 %collective-permute-start.8 = (f32[128,256]{1,0:T(8,128)}, f32[128,256]{1,0:T(8,128)S(1)}, u32[]{:S(2)}, u32[]{:S(2)}) collective-permute-start(f32[128,256]{1,0:T(8,128)} %get-tuple-element.29), channel_id=1, source_target_pairs={{0,2},{1,3},{2,0},{3,1},{4,6},{5,7},{6,4},{7,5},{8,10},{9,11},{10,... | collective-permute-start | bytes 393224 | tf_op jit(solution)/shard_map/ppermute | solution.py:13
  71.4 3.4 %collective-permute-done.22.rest_3_ = f32[3,128,256]{2,1,0:T(8,128)S(1)} collective-permute-done((f32[3,128,256]{2,1,0:T(8,128)S(1)}, f32[3,128,256]{2,1,0:T(8,128)S(1)}, u32[]{:S(2)}, u32[]{:S(2)}) %collective-permute-start.22) | collective-permute-done | bytes 393248 | tf_op jit(solution)/shard_map/ppermute | solution.py:13
  74.8 10.0 %collective-permute-start.9 = (f32[128,256]{1,0:T(8,128)}, f32[128,256]{1,0:T(8,128)S(1)}, u32[]{:S(2)}, u32[]{:S(2)}) collective-permute-start(f32[128,256]{1,0:T(8,128)} %get-tuple-element.28), channel_id=1, source_target_pairs={{0,1},{1,0},{2,3},{3,2},{4,5},{5,4},{6,7},{7,6},{8,9},{9,8},{10,11... | collective-permute-start | bytes 393224 | tf_op jit(solution)/shard_map/ppermute | solution.py:13
  84.8 4.5 %shard_map.69 = f32[512,256]{1,0:T(8,128)} custom-call(s32[2]{0:T(128)} %pad_add_fusion.place, f32[512,256]{1,0:T(8,128)} %own.4, f32[3,128,256]{2,1,0:T(8,128)} %copy-done.5, f32[3,128,256]{2,1,0:T(8,128)} %collective-permute-done.20.rest_1_, f32[3,128,256]{2,1,0:T(8,128)} %copy-done.10, f32[3,128,256]{2,1,0:T(8,128)} %copy-done.12, ...), custom_call_target="tpu_custom_call" | custom-call | flops 805306368 | bytes 3145728 | tf_op jit(solution)/shard_map/pallas_call | solution.py:132
  90.5 1.6 %collective-permute-start.15 = (f32[3,32,1024]{2,1,0:T(8,128)S(1)}, f32[3,32,1024]{2,1,0:T(8,128)S(1)}, u32[]{:S(2)}, u32[]{:S(2)}) collective-permute-start(f32[3,32,1024]{2,1,0:T(8,128)S(1)} %pad_maximum_fusion.8.rest_0_), channel_id=1, source_target_pairs={{0,8},{4,12},{8,0},{12,4},{1,9},{5,13},{9,1},{13,5},{2,10},{6,14},... | collective-permute-start | bytes 1179656 | tf_op jit(solution)/shard_map/ppermute | solution.py:13
  92.8 1.6 %collective-permute-start.16 = (f32[3,32,1024]{2,1,0:T(8,128)}, f32[3,32,1024]{2,1,0:T(8,128)}, u32[]{:S(2)}, u32[]{:S(2)}) collective-permute-start(f32[3,32,1024]{2,1,0:T(8,128)} %collective-permute-done.14.rest_1_), channel_id=1, source_target_pairs={{0,8},{4,12},{8,0},{12,4},{1,9},{5,13},{9,1},{13,5},{2,10},{6,14},... | collective-permute-start | bytes 1179656 | tf_op jit(solution)/shard_map/ppermute | solution.py:13
  95.6 7.0 %collective-permute-done.15.rest_2_ = f32[3,32,1024]{2,1,0:T(8,128)S(1)} collective-permute-done((f32[3,32,1024]{2,1,0:T(8,128)S(1)}, f32[3,32,1024]{2,1,0:T(8,128)S(1)}, u32[]{:S(2)}, u32[]{:S(2)}) %collective-permute-start.15) | collective-permute-done | bytes 393248 | tf_op jit(solution)/shard_map/ppermute | solution.py:13
  103.3 15.7 %collective-permute-done.16.rest_3_ = f32[3,32,1024]{2,1,0:T(8,128)} collective-permute-done((f32[3,32,1024]{2,1,0:T(8,128)}, f32[3,32,1024]{2,1,0:T(8,128)}, u32[]{:S(2)}, u32[]{:S(2)}) %collective-permute-start.16) | collective-permute-done | bytes 393248 | tf_op jit(solution)/shard_map/ppermute | solution.py:13
  119.0 4.3 %shard_map.70 = f32[4,128,256]{2,1,0:T(8,128)} custom-call(s32[2]{0:T(128)} %pad_add_fusion.place, f32[2,256,1024]{2,1,0:T(8,128)} %own.5, f32[3,32,1024]{2,1,0:T(8,128)} %copy-done.7, f32[3,32,1024]{2,1,0:T(8,128)} %collective-permute-done.14.rest_1_, f32[3,32,1024]{2,1,0:T(8,128)} %copy-done.14, f32[3,32,1024]{2,1,0:T(8,128)} %collective-permute-done.16.rest_3_, ...), custom_call_target="tpu_custom_call" | custom-call | flops 805306368 | bytes 2621440 | tf_op jit(solution)/shard_map/pallas_call | solution.py:132
  124.4 2.7 %collective-permute-start.25 = (f32[128,256]{1,0:T(8,128)S(1)}, f32[128,256]{1,0:T(8,128)S(1)}, u32[]{:S(2)}, u32[]{:S(2)}) collective-permute-start(f32[128,256]{1,0:T(8,128)S(1)} %get-tuple-element.33), channel_id=1, source_target_pairs={{0,3},{1,2},{2,1},{3,0},{4,7},{5,6},{6,5},{7,4},{8,11},{9,10},{10,... | collective-permute-start | bytes 393224 | tf_op jit(solution)/shard_map/ppermute | solution.py:13
  127.1 1.7 %collective-permute-start.27 = (f32[128,256]{1,0:T(8,128)S(1)}, f32[128,256]{1,0:T(8,128)S(1)}, u32[]{:S(2)}, u32[]{:S(2)}) collective-permute-start(f32[128,256]{1,0:T(8,128)S(1)} %get-tuple-element.31), channel_id=1, source_target_pairs={{0,1},{1,0},{2,3},{3,2},{4,5},{5,4},{6,7},{7,6},{8,9},{9,8},{10,11... | collective-permute-start | bytes 393224 | tf_op jit(solution)/shard_map/ppermute | solution.py:13
  130.3 2.4 %collective-permute-done.25 = f32[128,256]{1,0:T(8,128)S(1)} collective-permute-done((f32[128,256]{1,0:T(8,128)S(1)}, f32[128,256]{1,0:T(8,128)S(1)}, u32[]{:S(2)}, u32[]{:S(2)}) %collective-permute-start.25) | collective-permute-done | bytes 131104 | tf_op jit(solution)/shard_map/ppermute | solution.py:13
  133.2 4.8 %collective-permute-done.26 = f32[128,256]{1,0:T(8,128)S(1)} collective-permute-done((f32[128,256]{1,0:T(8,128)S(1)}, f32[128,256]{1,0:T(8,128)S(1)}, u32[]{:S(2)}, u32[]{:S(2)}) %collective-permute-start.26) | collective-permute-done | bytes 131104 | tf_op jit(solution)/shard_map/ppermute | solution.py:13
  141.7 6.3 %collective-permute-done.34.rest_3_ = f32[3,64,512]{2,1,0:T(8,128)} collective-permute-done((f32[3,64,512]{2,1,0:T(8,128)}, f32[3,64,512]{2,1,0:T(8,128)}, u32[]{:S(2)}, u32[]{:S(2)}) %collective-permute-start.34) | collective-permute-done | bytes 393248 | tf_op jit(solution)/shard_map/ppermute | solution.py:13
  148.0 4.6 %shard_map.71 = f32[256,256]{1,0:T(8,128)} custom-call(s32[2]{0:T(128)} %pad_add_fusion.place, f32[256,512]{1,0:T(8,128)} %bitcast.69, f32[3,64,512]{2,1,0:T(8,128)} %copy-done.4, f32[3,64,512]{2,1,0:T(8,128)} %copy-done.11, f32[3,64,512]{2,1,0:T(8,128)} %collective-permute-done.33.rest_2_, f32[3,64,512]{2,1,0:T(8,128)} %collective-permute-done.34.rest_3_, ...), custom_call_target="tpu_custom_call" | custom-call | flops 805306368 | bytes 3932160 | tf_op jit(solution)/shard_map/pallas_call | solution.py:132
  154.0 1.5 pad_maximum_fusion
  (113 shorter events, 29.4 us)
Async XLA Ops:
  1.7 9.7 %collective-permute-start = (f32[32,1024]{1,0:T(8,128)S(1)}, f32[32,1024]{1,0:T(8,128)}, u32[]{:S(2)}, u32[]{:S(2)}) collective-permute-start(f32[32,1024]{1,0:T(8,128)S(1)} %get-tuple-element.2), channel_id=1, source_target_pairs={{0,1},{1,0},{2,3},{3,2},{4,5},{5,4},{6,7},{7,6},{8,9},{9,8},{10,11... | collective-permute-start | bytes 393224 | tf_op jit(solution)/shard_map/ppermute | solution.py:13
  4.9 13.0 %collective-permute-start.1 = (f32[32,1024]{1,0:T(8,128)S(1)}, f32[32,1024]{1,0:T(8,128)}, u32[]{:S(2)}, u32[]{:S(2)}) collective-permute-start(f32[32,1024]{1,0:T(8,128)S(1)} %get-tuple-element.2), channel_id=1, source_target_pairs={{0,2},{1,3},{2,0},{3,1},{4,6},{5,7},{6,4},{7,5},{8,10},{9,11},{10,... | collective-permute-start | bytes 393224 | tf_op jit(solution)/shard_map/ppermute | solution.py:13
  7.4 10.5 %collective-permute-start.2 = (f32[32,1024]{1,0:T(8,128)S(1)}, f32[32,1024]{1,0:T(8,128)S(1)}, u32[]{:S(2)}, u32[]{:S(2)}) collective-permute-start(f32[32,1024]{1,0:T(8,128)S(1)} %get-tuple-element.2), channel_id=1, source_target_pairs={{0,3},{1,2},{2,1},{3,0},{4,7},{5,6},{6,5},{7,4},{8,11},{9,10},{10,... | collective-permute-start | bytes 393224 | tf_op jit(solution)/shard_map/ppermute | solution.py:13
  9.7 23.6 %collective-permute-start.6 = (f32[512,256]{1,0:T(8,128)}, f32[512,256]{1,0:T(8,128)S(1)}, u32[]{:S(2)}, u32[]{:S(2)}) collective-permute-start(f32[512,256]{1,0:T(8,128)} %get-tuple-element.15), channel_id=1, source_target_pairs={{0,16},{16,0},{1,17},{17,1},{2,18},{18,2},{3,19},{19,3},{4,20},{20... | collective-permute-start | bytes 1572872 | tf_op jit(solution)/shard_map/ppermute | solution.py:13
  10.4 10.8 %collective-permute-start.17 = (f32[128,256]{1,0:T(8,128)}, f32[128,256]{1,0:T(8,128)S(1)}, u32[]{:S(2)}, u32[]{:S(2)}) collective-permute-start(f32[128,256]{1,0:T(8,128)} %constant_dynamic-slice_fusion.1), channel_id=1, source_target_pairs={{0,1},{1,0},{2,3},{3,2},{4,5},{5,4},{6,7},{7,6},{8,9},{9,8},{10,11... | collective-permute-start | bytes 393224 | tf_op jit(solution)/shard_map/ppermute | solution.py:13
  11.4 11.1 %collective-permute-start.11 = (f32[32,1024]{1,0:T(8,128)S(1)}, f32[32,1024]{1,0:T(8,128)S(1)}, u32[]{:S(2)}, u32[]{:S(2)}) collective-permute-start(f32[32,1024]{1,0:T(8,128)S(1)} %bitcast.78), channel_id=1, source_target_pairs={{0,1},{1,0},{2,3},{3,2},{4,5},{5,4},{6,7},{7,6},{8,9},{9,8},{10,11... | collective-permute-start | bytes 393224 | tf_op jit(solution)/shard_map/ppermute | solution.py:13
  17.9 7.1 %collective-permute-start.29 = (f32[64,512]{1,0:T(8,128)S(1)}, f32[64,512]{1,0:T(8,128)S(1)}, u32[]{:S(2)}, u32[]{:S(2)}) collective-permute-start(f32[64,512]{1,0:T(8,128)S(1)} %bitcast.79), channel_id=1, source_target_pairs={{0,1},{1,0},{2,3},{3,2},{4,5},{5,4},{6,7},{7,6},{8,9},{9,8},{10,11... | collective-permute-start | bytes 393224 | tf_op jit(solution)/shard_map/ppermute | solution.py:13
  19.6 12.3 %collective-permute-start.3 = (f32[3,32,1024]{2,1,0:T(8,128)S(1)}, f32[3,32,1024]{2,1,0:T(8,128)}, u32[]{:S(2)}, u32[]{:S(2)}) collective-permute-start(f32[3,32,1024]{2,1,0:T(8,128)S(1)} %pad_maximum_fusion.7.rest_0_), channel_id=1, source_target_pairs={{0,4},{4,0},{8,12},{12,8},{1,5},{5,1},{9,13},{13,9},{2,6},{6,2},{1... | collective-permute-start | bytes 1179656 | tf_op jit(solution)/shard_map/ppermute | solution.py:13
  21.2 6.5 %collective-permute-start.18 = (f32[2,128,256]{2,1,0:T(8,128)S(1)}, f32[2,128,256]{2,1,0:T(8,128)}, u32[]{:S(2)}, u32[]{:S(2)}) collective-permute-start(f32[2,128,256]{2,1,0:T(8,128)S(1)} %pad_maximum_fusion.12), channel_id=1, source_target_pairs={{1,2},{2,1},{5,6},{6,5},{9,10},{10,9},{13,14},{14,13},{17,18},{18,... | collective-permute-start | bytes 786440 | tf_op jit(solution)/shard_map/ppermute | solution.py:46
  27.7 20.3 %collective-permute-start.4 = (f32[3,32,1024]{2,1,0:T(8,128)S(1)}, f32[3,32,1024]{2,1,0:T(8,128)S(1)}, u32[]{:S(2)}, u32[]{:S(2)}) collective-permute-start(f32[3,32,1024]{2,1,0:T(8,128)S(1)} %pad_maximum_fusion.7.rest_0_), channel_id=1, source_target_pairs={{0,8},{4,12},{8,0},{12,4},{1,9},{5,13},{9,1},{13,5},{2,10},{6,14},... | collective-permute-start | bytes 1179656 | tf_op jit(solution)/shard_map/ppermute | solution.py:13
  29.4 16.0 %collective-permute-start.19 = (f32[2,128,256]{2,1,0:T(8,128)}, f32[2,128,256]{2,1,0:T(8,128)S(1)}, u32[]{:S(2)}, u32[]{:S(2)}) collective-permute-start(f32[2,128,256]{2,1,0:T(8,128)} %collective-permute-done.18), channel_id=1, source_target_pairs={{1,0},{2,3},{5,4},{6,7},{9,8},{10,11},{13,12},{14,15},{17,16},{18,... | collective-permute-start | bytes 786440 | tf_op jit(solution)/shard_map/ppermute | solution.py:47
  30.7 23.0 %collective-permute-start.13 = (f32[2,32,1024]{2,1,0:T(8,128)}, f32[2,32,1024]{2,1,0:T(8,128)}, u32[]{:S(2)}, u32[]{:S(2)}) collective-permute-start(f32[2,32,1024]{2,1,0:T(8,128)} %collective-permute-done.12), channel_id=1, source_target_pairs={{1,0},{2,3},{5,4},{6,7},{9,8},{10,11},{13,12},{14,15},{17,16},{18,... | collective-permute-start | bytes 786440 | tf_op jit(solution)/shard_map/ppermute | solution.py:47
  32.0 57.3 %collective-permute-start.31 = (f32[2,64,512]{2,1,0:T(8,128)}, f32[2,64,512]{2,1,0:T(8,128)}, u32[]{:S(2)}, u32[]{:S(2)}) collective-permute-start(f32[2,64,512]{2,1,0:T(8,128)} %collective-permute-done.30), channel_id=1, source_target_pairs={{1,0},{2,3},{5,4},{6,7},{9,8},{10,11},{13,12},{14,15},{17,16},{18,... | collective-permute-start | bytes 786440 | tf_op jit(solution)/shard_map/ppermute | solution.py:47
  33.3 16.0 %collective-permute-start.5 = (f32[3,32,1024]{2,1,0:T(8,128)}, f32[3,32,1024]{2,1,0:T(8,128)}, u32[]{:S(2)}, u32[]{:S(2)}) collective-permute-start(f32[3,32,1024]{2,1,0:T(8,128)} %collective-permute-done.3.rest_1_), channel_id=1, source_target_pairs={{0,8},{4,12},{8,0},{12,4},{1,9},{5,13},{9,1},{13,5},{2,10},{6,14},... | collective-permute-start | bytes 1179656 | tf_op jit(solution)/shard_map/ppermute | solution.py:13
  46.4 11.8 %collective-permute-start.21 = (f32[3,128,256]{2,1,0:T(8,128)S(1)}, f32[3,128,256]{2,1,0:T(8,128)S(1)}, u32[]{:S(2)}, u32[]{:S(2)}) collective-permute-start(f32[3,128,256]{2,1,0:T(8,128)S(1)} %pad_maximum_fusion.9.rest_0_), channel_id=1, source_target_pairs={{0,8},{4,12},{8,0},{12,4},{1,9},{5,13},{9,1},{13,5},{2,10},{6,14},... | collective-permute-start | bytes 1179656 | tf_op jit(solution)/shard_map/ppermute | solution.py:13
  48.8 16.3 %collective-permute-start.20 = (f32[3,128,256]{2,1,0:T(8,128)S(1)}, f32[3,128,256]{2,1,0:T(8,128)}, u32[]{:S(2)}, u32[]{:S(2)}) collective-permute-start(f32[3,128,256]{2,1,0:T(8,128)S(1)} %pad_maximum_fusion.9.rest_0_), channel_id=1, source_target_pairs={{0,4},{4,0},{8,12},{12,8},{1,5},{5,1},{9,13},{13,9},{2,6},{6,2},{1... | collective-permute-start | bytes 1179656 | tf_op jit(solution)/shard_map/ppermute | solution.py:13
  53.6 9.7 %collective-permute-start.23 = (f32[4,128,256]{2,1,0:T(8,128)}, f32[4,128,256]{2,1,0:T(8,128)S(1)}, u32[]{:S(2)}, u32[]{:S(2)}) collective-permute-start(f32[4,128,256]{2,1,0:T(8,128)} %shard_map.68), channel_id=1, source_target_pairs={{0,16},{16,0},{1,17},{17,1},{2,18},{18,2},{3,19},{19,3},{4,20},{20... | collective-permute-start | bytes 1572872 | tf_op jit(solution)/shard_map/ppermute | solution.py:13
  54.9 37.9 %collective-permute-start.14 = (f32[3,32,1024]{2,1,0:T(8,128)S(1)}, f32[3,32,1024]{2,1,0:T(8,128)}, u32[]{:S(2)}, u32[]{:S(2)}) collective-permute-start(f32[3,32,1024]{2,1,0:T(8,128)S(1)} %pad_maximum_fusion.8.rest_0_), channel_id=1, source_target_pairs={{0,4},{4,0},{8,12},{12,8},{1,5},{5,1},{9,13},{13,9},{2,6},{6,2},{1... | collective-permute-start | bytes 1179656 | tf_op jit(solution)/shard_map/ppermute | solution.py:13
  58.2 32.3 %collective-permute-start.7 = (f32[128,256]{1,0:T(8,128)}, f32[128,256]{1,0:T(8,128)S(1)}, u32[]{:S(2)}, u32[]{:S(2)}) collective-permute-start(f32[128,256]{1,0:T(8,128)} %get-tuple-element.30), channel_id=1, source_target_pairs={{0,3},{1,2},{2,1},{3,0},{4,7},{5,6},{6,5},{7,4},{8,11},{9,10},{10,... | collective-permute-start | bytes 393224 | tf_op jit(solution)/shard_map/ppermute | solution.py:13
  63.4 11.5 %collective-permute-start.22 = (f32[3,128,256]{2,1,0:T(8,128)S(1)}, f32[3,128,256]{2,1,0:T(8,128)S(1)}, u32[]{:S(2)}, u32[]{:S(2)}) collective-permute-start(f32[3,128,256]{2,1,0:T(8,128)S(1)} %collective-permute-done.21.rest_2_), channel_id=1, source_target_pairs={{0,4},{4,0},{8,12},{12,8},{1,5},{5,1},{9,13},{13,9},{2,6},{6,2},{1... | collective-permute-start | bytes 1179656 | tf_op jit(solution)/shard_map/ppermute | solution.py:13
  65.1 27.0 %collective-permute-start.8 = (f32[128,256]{1,0:T(8,128)}, f32[128,256]{1,0:T(8,128)S(1)}, u32[]{:S(2)}, u32[]{:S(2)}) collective-permute-start(f32[128,256]{1,0:T(8,128)} %get-tuple-element.29), channel_id=1, source_target_pairs={{0,2},{1,3},{2,0},{3,1},{4,6},{5,7},{6,4},{7,5},{8,10},{9,11},{10,... | collective-permute-start | bytes 393224 | tf_op jit(solution)/shard_map/ppermute | solution.py:13
  74.8 17.8 %collective-permute-start.9 = (f32[128,256]{1,0:T(8,128)}, f32[128,256]{1,0:T(8,128)S(1)}, u32[]{:S(2)}, u32[]{:S(2)}) collective-permute-start(f32[128,256]{1,0:T(8,128)} %get-tuple-element.28), channel_id=1, source_target_pairs={{0,1},{1,0},{2,3},{3,2},{4,5},{5,4},{6,7},{7,6},{8,9},{9,8},{10,11... | collective-permute-start | bytes 393224 | tf_op jit(solution)/shard_map/ppermute | solution.py:13
  90.5 12.1 %collective-permute-start.15 = (f32[3,32,1024]{2,1,0:T(8,128)S(1)}, f32[3,32,1024]{2,1,0:T(8,128)S(1)}, u32[]{:S(2)}, u32[]{:S(2)}) collective-permute-start(f32[3,32,1024]{2,1,0:T(8,128)S(1)} %pad_maximum_fusion.8.rest_0_), channel_id=1, source_target_pairs={{0,8},{4,12},{8,0},{12,4},{1,9},{5,13},{9,1},{13,5},{2,10},{6,14},... | collective-permute-start | bytes 1179656 | tf_op jit(solution)/shard_map/ppermute | solution.py:13
  92.1 37.5 %collective-permute-start.33 = (f32[3,64,512]{2,1,0:T(8,128)S(1)}, f32[3,64,512]{2,1,0:T(8,128)}, u32[]{:S(2)}, u32[]{:S(2)}) collective-permute-start(f32[3,64,512]{2,1,0:T(8,128)S(1)} %pad_maximum_fusion.10.rest_0_), channel_id=1, source_target_pairs={{0,8},{4,12},{8,0},{12,4},{1,9},{5,13},{9,1},{13,5},{2,10},{6,14},... | collective-permute-start | bytes 1179656 | tf_op jit(solution)/shard_map/ppermute | solution.py:13
  92.7 47.6 %collective-permute-start.10 = (f32[128,1024]{1,0:T(8,128)S(1)}, f32[128,1024]{1,0:T(8,128)S(1)}, u32[]{:S(2)}, u32[]{:S(2)}) collective-permute-start(f32[128,1024]{1,0:T(8,128)S(1)} %pad_maximum_fusion.5), channel_id=1, source_target_pairs={{0,16},{16,0},{1,17},{17,1},{2,18},{18,2},{3,19},{19,3},{4,20},{20... | collective-permute-start | bytes 1572872 | tf_op jit(solution)/shard_map/ppermute | solution.py:13
  92.8 26.2 %collective-permute-start.16 = (f32[3,32,1024]{2,1,0:T(8,128)}, f32[3,32,1024]{2,1,0:T(8,128)}, u32[]{:S(2)}, u32[]{:S(2)}) collective-permute-start(f32[3,32,1024]{2,1,0:T(8,128)} %collective-permute-done.14.rest_1_), channel_id=1, source_target_pairs={{0,8},{4,12},{8,0},{12,4},{1,9},{5,13},{9,1},{13,5},{2,10},{6,14},... | collective-permute-start | bytes 1179656 | tf_op jit(solution)/shard_map/ppermute | solution.py:13
  124.4 8.3 %collective-permute-start.25 = (f32[128,256]{1,0:T(8,128)S(1)}, f32[128,256]{1,0:T(8,128)S(1)}, u32[]{:S(2)}, u32[]{:S(2)}) collective-permute-start(f32[128,256]{1,0:T(8,128)S(1)} %get-tuple-element.33), channel_id=1, source_target_pairs={{0,3},{1,2},{2,1},{3,0},{4,7},{5,6},{6,5},{7,4},{8,11},{9,10},{10,... | collective-permute-start | bytes 393224 | tf_op jit(solution)/shard_map/ppermute | solution.py:13
  127.1 10.9 %collective-permute-start.26 = (f32[128,256]{1,0:T(8,128)S(1)}, f32[128,256]{1,0:T(8,128)S(1)}, u32[]{:S(2)}, u32[]{:S(2)}) collective-permute-start(f32[128,256]{1,0:T(8,128)S(1)} %get-tuple-element.32), channel_id=1, source_target_pairs={{0,2},{1,3},{2,0},{3,1},{4,6},{5,7},{6,4},{7,5},{8,10},{9,11},{10,... | collective-permute-start | bytes 393224 | tf_op jit(solution)/shard_map/ppermute | solution.py:13
  127.1 10.9 %collective-permute-start.27 = (f32[128,256]{1,0:T(8,128)S(1)}, f32[128,256]{1,0:T(8,128)S(1)}, u32[]{:S(2)}, u32[]{:S(2)}) collective-permute-start(f32[128,256]{1,0:T(8,128)S(1)} %get-tuple-element.31), channel_id=1, source_target_pairs={{0,1},{1,0},{2,3},{3,2},{4,5},{5,4},{6,7},{7,6},{8,9},{9,8},{10,11... | collective-permute-start | bytes 393224 | tf_op jit(solution)/shard_map/ppermute | solution.py:13
  129.7 12.1 %collective-permute-start.32 = (f32[3,64,512]{2,1,0:T(8,128)S(1)}, f32[3,64,512]{2,1,0:T(8,128)S(1)}, u32[]{:S(2)}, u32[]{:S(2)}) collective-permute-start(f32[3,64,512]{2,1,0:T(8,128)S(1)} %pad_maximum_fusion.10.rest_0_), channel_id=1, source_target_pairs={{0,4},{4,0},{8,12},{12,8},{1,5},{5,1},{9,13},{13,9},{2,6},{6,2},{1... | collective-permute-start | bytes 1179656 | tf_op jit(solution)/shard_map/ppermute | solution.py:13
  132.7 15.3 %collective-permute-start.34 = (f32[3,64,512]{2,1,0:T(8,128)}, f32[3,64,512]{2,1,0:T(8,128)}, u32[]{:S(2)}, u32[]{:S(2)}) collective-permute-start(f32[3,64,512]{2,1,0:T(8,128)} %collective-permute-done.33.rest_2_), channel_id=1, source_target_pairs={{0,4},{4,0},{8,12},{12,8},{1,5},{5,1},{9,13},{13,9},{2,6},{6,2},{1... | collective-permute-start | bytes 1179656 | tf_op jit(solution)/shard_map/ppermute | solution.py:13
  139.9 12.8 %collective-permute-start.28 = (f32[128,1024]{1,0:T(8,128)}, f32[128,1024]{1,0:T(8,128)}, u32[]{:S(2)}, u32[]{:S(2)}) collective-permute-start(f32[128,1024]{1,0:T(8,128)} %pad_maximum_fusion.6), channel_id=1, source_target_pairs={{0,16},{16,0},{1,17},{17,1},{2,18},{18,2},{3,19},{19,3},{4,20},{20... | collective-permute-start | bytes 1572872 | tf_op jit(solution)/shard_map/ppermute | solution.py:13
  (20 other events, 211.2 us)

commit v2 on v1

--- a/solution.py
+++ b/solution.py
@@ -41,7 +41,8 @@
 def from_depth(part, relay):
     size = lax.axis_size("depth")
     if not (relay and size == 4):
-        return jnp.stack([exchange(part, "depth", k) for k in range(1, size)])
+        parts = [exchange(part, "depth", k) for k in range(1, size)]
+        return jnp.stack(parts)
     near = exchange(part, "depth", 1)
     across = lax.ppermute(jnp.stack([part, near]), "depth", [(1, 2), (2, 1)])
     handed = lax.ppermute(across, "depth", [(1, 0), (2, 3)])
@@ -49,6 +50,30 @@
     outer = (index == 0) | (index == size - 1)
     far = [jnp.where(outer, handed[0], across[1]), jnp.where(outer, handed[1], across[0])]
     return jnp.stack([near] + far)
+
+
+def pack_lower(parts):
+    index = lax.axis_index("depth")
+    size = len(parts) + 1
+    packed = []
+    for n in range(1, size):
+        pick = None
+        for d in range(size):
+            source = n - 1 if n - 1 < d else n
+            part = parts[(source ^ d) - 1][: n + 1]
+            pick = part if pick is None else jnp.where(index == d, part, pick)
+        packed.append(pick)
+    return jnp.concatenate(packed)
+
+
+def gather_inverse(own, low_first):
+    part = own_part(own, 0, "col")
+    size = lax.axis_size("depth")
+    if part.shape[0] % 8:
+        return from_columns(from_depth(part, False), low_first)
+    part = part.reshape(part.shape[0], size, -1).transpose(1, 0, 2)
+    parts = [exchange(part, "depth", k) for k in range(1, size)]
+    return from_columns(pack_lower(parts), low_first)
 
 
 def from_columns(parts, low_first):
@@ -80,23 +105,28 @@
     return dot(left_high, right_high) + (dot(left_high, right_low) + dot(left_low, right_high))
 
 
-def solve_kernel(place, own, *rest):
+def solve_kernel(blocks, place, own, *rest):
     *parts, rhs, out = rest
-    right = halves(rhs[...])
-    count, size, depth = parts[0].shape
-    out[0] = product(own[0], right)
-    left = jnp.concatenate([part[...].reshape(count * size, depth) for part in parts])
-    rows = product(left, right)
-    for k in range(len(parts)):
-        at = pl.multiple_of((place[1] ^ k) * size, size)
-        for j in range(count):
-            from_row = (k * count + j) * size
-            out[j + 1, pl.ds(at, size), :] = rows[from_row : from_row + size]
-
-
-def update_kernel(quarters, place, own, *rest):
-    *solved, base, out = rest[quarters:]
-    parts = rest[:quarters]
+    high, low = halves(rhs[...])
+    _, size, width = parts[0].shape
+    out[0] = product(own[0], (high, low))
+    first = 0
+    for n in range(1, blocks):
+        chunks = range(first, first + n + 1)
+        first += n + 1
+        left = jnp.concatenate([jnp.concatenate([part[c] for c in chunks], axis=1) for part in parts])
+        depth = (n + 1) * width
+        rows = product(left, (high[:depth], low[:depth]))
+        source = n - 1 + (n - 1 >= place[2]).astype(jnp.int32)
+        for k in range(len(parts)):
+            at = pl.multiple_of((place[1] ^ k) * size, size)
+            out[source ^ place[2], pl.ds(at, size), :] = rows[k * size : (k + 1) * size]
+
+
+def update_kernel(quarters, place, *rest):
+    *rest, base, out = rest
+    sections = (len(rest) - quarters) // 2
+    own, parts, solved = rest[:sections], rest[sections : sections + quarters], rest[sections + quarters :]
     count, size, _ = parts[0].shape
     depth = solved[0].shape[1]
     near = far = None
@@ -105,7 +135,7 @@
         for j in range(count + 1):
             right = halves(blocks[j])
             if j == 0:
-                term = product(own[:, at], right)
+                term = product(own[s][...], right)
                 near = term if near is None else near + term
             else:
                 left = jnp.concatenate([part[j - 1][:, at] for part in parts])
@@ -139,6 +169,7 @@
             out_specs=whole(out),
         ),
         cost_estimate=cost(flops, operands[1:]),
+        compiler_params=pltpu.CompilerParams(vmem_limit_bytes=24 * 2**20),
     )(place, *operands)
 
 
@@ -149,15 +180,16 @@
 def solve(place, section, inverses, parts, rhs):
     rows = inverses.shape[1] // lax.axis_size("row")
     nb, cols = rhs.shape
-    count, size, _ = parts[0].shape
-    if size % 8:
+    blocks = nb // inverses.shape[1]
+    if (rows // len(parts)) % 8:
         own = plain_product(own_part(inverses[section], 0, "row"), rhs)
         ordered = jnp.concatenate(in_order(list(parts), place[1]), axis=1)
-        return jnp.stack([own] + [plain_product(ordered[j], rhs) for j in range(count)])
+        return jnp.stack([own] + [plain_product(ordered[j], rhs) for j in range(blocks - 1)])
     spec = pl.BlockSpec((1, rows, nb), lambda i, p: (section, p[0], 0))
-    shape = (count + 1, rows, cols)
-    flops = 6 * (count + 1) * rows * nb * cols
-    return call_kernel(solve_kernel, place, spec, (inverses, *parts, rhs), shape, flops)
+    shape = (blocks, rows, cols)
+    flops = 6 * blocks * rows * nb * cols
+    kernel = functools.partial(solve_kernel, blocks)
+    return call_kernel(kernel, place, spec, (inverses, *parts, rhs), shape, flops)
 
 
 def update(place, own, parts, solved, base):
@@ -167,13 +199,13 @@
         ordered = jnp.concatenate(in_order(list(parts), place[1]), axis=1)
         for s, blocks in enumerate(solved):
             at = slice(s * depth, (s + 1) * depth)
-            base = base - plain_product(own[:, at], blocks[0])
+            base = base - plain_product(own[s], blocks[0])
             for j in range(count):
                 base = base - plain_product(ordered[j][:, at], blocks[j + 1])
         return base
     kernel = functools.partial(update_kernel, len(parts))
-    flops = 6 * own.size * (count + 1) * base.shape[1]
-    return call_kernel(kernel, place, whole(own), (own, *parts, *solved, base), base.shape, flops)
+    flops = 6 * sum(a.size for a in own) * (count + 1) * base.shape[1]
+    return call_kernel(kernel, place, whole(own[0]), (*own, *parts, *solved, base), base.shape, flops)
 
 
 def to_output(parts):
@@ -185,20 +217,20 @@
 
 
 def steps(head_rhs, head_factor, inverses, trail_factor, trail_rhs):
-    place = jnp.stack([lax.axis_index("row"), lax.axis_index("col")])
+    place = jnp.stack([lax.axis_index(axis) for axis in ("row", "col", "depth")])
     lower = own_part(inverses, 1, "row")
     count = trail_factor.shape[0]
-    trail_own = trail_factor.reshape(count, -1)
+    trail_own = [trail_factor[:, section, :] for section in range(trail_factor.shape[1])]
     trail_part = own_part(trail_factor, 0, "col").reshape(count // lax.axis_size("col"), -1)
-    first_factor = gather_factor(lower[0], True, False)
-    mid_factor = gather_factor(head_factor, False, True)
-    second_factor = gather_factor(lower[1], True, True)
-    trail_parts = from_columns(from_depth(trail_part, True), False)
+    first_factor = gather_inverse(lower[0], True)
+    mid_factor = gather_factor(head_factor, False, False)
+    second_factor = gather_inverse(lower[1], True)
+    trail_parts = from_columns(from_depth(trail_part, False), True)
 
     rhs = share_rows(head_rhs[0], 0)
     first_part = solve(place, 0, inverses, first_factor, rhs)
     first = share_rows(first_part, 1)
-    second_rhs = update(place, head_factor, mid_factor, [first], head_rhs[1])
+    second_rhs = update(place, [head_factor], mid_factor, [first], head_rhs[1])
     second_rhs = share_rows(second_rhs, 0)
     second_part = solve(place, 1, inverses, second_factor, second_rhs)
     second = share_rows(second_part, 1)

time: 156 us -> 150 us (0.962)
  waiting for transfers between devices: 55.8 us -> 73 us
  other arithmetic: 16.1 us -> 6.37 us
  Pallas kernels: 17.7 us -> 8.44 us
  starting transfers between devices: 54.9 us -> 52.7 us
  local copies, waits for them, and re-layouts: 9.97 us -> 7.95 us
    ppermute x30 -> x36, waiting for transfers between devices: 45.3 us -> 73 us  [exchange(): return lax.ppermute(value, axis, pairs)]
    ppermute x6 -> x0, waiting for transfers between devices: 10.5 us -> none  [the longest x3 10.5 us: from_depth(): handed = lax.ppermute(across, 'depth', [(1, 0), (2, 3)])]
    pallas_call x4, Pallas kernels: 17.7 us -> 8.44 us  [call_kernel(): pl.pallas_call(kernel, out_shape=out, grid_spec=pltpu.PrefetchScalarGridS...]
    ppermute x6 -> x0, starting transfers between devices: 7.96 us -> none  [the longest x3 4.1 us: from_depth(): across = lax.ppermute(jnp.stack([part, near]), 'depth', [(1, 2), (2, 1)])]
    ppermute x30 -> x36, starting transfers between devices: 46.9 us -> 52.7 us  [exchange(): return lax.ppermute(value, axis, pairs)]
    concatenate x4, other arithmetic: 4.25 us -> 0.3 us  [share_rows(): jnp.concatenate([jnp.where(odd, other, value), jnp.where(odd, value, othe...]
    select_n x3 -> x6, other arithmetic: 3.37 us -> 0.11 us  [pack_lower(): pick = part if pick is None else jnp.where(index == d, part, pick)]
    unnamed x34 -> x25, local copies, waits for them, and re-layouts: 3.03 us -> 0.63 us
  transfers between devices with their start and end apart: 36 -> 36, of which waited for: 9 -> 16; matrix products, arithmetic and copies ran while one was open for 13% -> 7% of each run, Pallas kernels for 11% -> 6%
where the time goes in v2:
time: 150 us
  waiting for transfers between devices  73 us (49%)
  starting transfers between devices  52.7 us (35%)
  Pallas kernels  8.44 us (6%)
  local copies, waits for them, and re-layouts  7.95 us (5%)
  other arithmetic  6.37 us (4%)
    ppermute x36, waiting for transfers between devices, exchange(): return lax.ppermute(value, axis, pairs)  73 us
    ppermute x36, starting transfers between devices, exchange(): return lax.ppermute(value, axis, pairs)  52.7 us
    pallas_call x4, Pallas kernels, call_kernel(): pl.pallas_call(kernel, out_shape=out, grid_spec=pltpu.PrefetchScalarGridS...  8.44 us
  transfers between devices with their start and end apart: 36, of which 16 were waited for; matrix products, arithmetic and copies ran while one was open for 7% of the time, Pallas kernels for 6%

profile of v2, /device:TPU:0, one launch (start us, length us, event | category | flops | bytes accessed | tf_op | source)
XLA Modules:
  0.0 149.5 jit_solution(1182705231845177658)
XLA Ops:
  1.7 5.1 %collective-permute-start = (f32[4,32,256]{2,1,0:T(8,128)S(1)}, f32[4,32,256]{2,1,0:T(8,128)S(1)}, u32[]{:S(2)}, u32[]{:S(2)}) collective-permute-start(f32[4,32,256]{2,1,0:T(8,128)S(1)} %bitcast.77), channel_id=1, source_target_pairs={{0,3},{1,2},{2,1},{3,0},{4,7},{5,6},{6,5},{7,4},{8,11},{9,10},{10,... | collective-permute-start | bytes 393224 | tf_op jit(solution)/shard_map/ppermute | solution.py:13
  9.9 2.9 %collective-permute-start.18 = (f32[128,256]{1,0:T(8,128)S(1)}, f32[128,256]{1,0:T(8,128)S(1)}, u32[]{:S(2)}, u32[]{:S(2)}) collective-permute-start(f32[128,256]{1,0:T(8,128)S(1)} %constant_dynamic-slice_fusion.1), channel_id=1, source_target_pairs={{0,2},{1,3},{2,0},{3,1},{4,6},{5,7},{6,4},{7,5},{8,10},{9,11},{10,... | collective-permute-start | bytes 393224 | tf_op jit(solution)/shard_map/ppermute | solution.py:13
  12.8 2.2 %slice_bitcast_fusion = (f32[512,256]{1,0:T(8,128)}, f32[512,256]{1,0:T(8,128)}) fusion(f32[2,512,256]{2,1,0:T(8,128)} %param.5), kind=kLoop, calls=%fused_computation.9 | loop fusion | bytes 2097152 | tf_op jit(solution)/shard_map/squeeze | solution.py:233
  16.3 3.5 %collective-permute-done.1 = f32[4,32,256]{2,1,0:T(8,128)S(1)} collective-permute-done((f32[4,32,256]{2,1,0:T(8,128)S(1)}, f32[4,32,256]{2,1,0:T(8,128)S(1)}, u32[]{:S(2)}, u32[]{:S(2)}) %collective-permute-start.1) | collective-permute-done | bytes 131104 | tf_op jit(solution)/shard_map/ppermute | solution.py:13
  19.8 2.1 %collective-permute-start.11 = (f32[4,32,256]{2,1,0:T(8,128)S(1)}, f32[4,32,256]{2,1,0:T(8,128)S(1)}, u32[]{:S(2)}, u32[]{:S(2)}) collective-permute-start(f32[4,32,256]{2,1,0:T(8,128)S(1)} %bitcast.80), channel_id=1, source_target_pairs={{0,3},{1,2},{2,1},{3,0},{4,7},{5,6},{6,5},{7,4},{8,11},{9,10},{10,... | collective-permute-start | bytes 393224 | tf_op jit(solution)/shard_map/ppermute | solution.py:13
  22.0 6.3 %collective-permute-done.11 = f32[4,32,256]{2,1,0:T(8,128)S(1)} collective-permute-done((f32[4,32,256]{2,1,0:T(8,128)S(1)}, f32[4,32,256]{2,1,0:T(8,128)S(1)}, u32[]{:S(2)}, u32[]{:S(2)}) %collective-permute-start.11) | collective-permute-done | bytes 131104 | tf_op jit(solution)/shard_map/ppermute | solution.py:13
  28.2 10.9 %collective-permute-start.13 = (f32[4,32,256]{2,1,0:T(8,128)S(1)}, f32[4,32,256]{2,1,0:T(8,128)S(1)}, u32[]{:S(2)}, u32[]{:S(2)}) collective-permute-start(f32[4,32,256]{2,1,0:T(8,128)S(1)} %bitcast.82), channel_id=1, source_target_pairs={{0,1},{1,0},{2,3},{3,2},{4,5},{5,4},{6,7},{7,6},{8,9},{9,8},{10,11... | collective-permute-start | bytes 393224 | tf_op jit(solution)/shard_map/ppermute | solution.py:13
  40.7 3.0 %collective-permute-start.30 = (f32[64,512]{1,0:T(8,128)S(1)}, f32[64,512]{1,0:T(8,128)S(1)}, u32[]{:S(2)}, u32[]{:S(2)}) collective-permute-start(f32[64,512]{1,0:T(8,128)S(1)} %bitcast.75), channel_id=1, source_target_pairs={{0,2},{1,3},{2,0},{3,1},{4,6},{5,7},{6,4},{7,5},{8,10},{9,11},{10,... | collective-permute-start | bytes 393224 | tf_op jit(solution)/shard_map/ppermute | solution.py:13
  43.8 1.5 collective-permute-start.3
  46.8 5.9 %collective-permute-done.3.rest_1_ = f32[9,32,256]{2,1,0:T(8,128)S(1)} collective-permute-done((f32[9,32,256]{2,1,0:T(8,128)S(1)}, f32[9,32,256]{2,1,0:T(8,128)S(1)}, u32[]{:S(2)}, u32[]{:S(2)}) %collective-permute-start.3) | collective-permute-done | bytes 294944 | tf_op jit(solution)/shard_map/ppermute | solution.py:13
  52.6 1.5 %collective-permute-start.4 = (f32[9,32,256]{2,1,0:T(8,128)S(1)}, f32[9,32,256]{2,1,0:T(8,128)S(1)}, u32[]{:S(2)}, u32[]{:S(2)}) collective-permute-start(f32[9,32,256]{2,1,0:T(8,128)S(1)} %pad_maximum_fusion.9.rest_0_), channel_id=1, source_target_pairs={{0,8},{4,12},{8,0},{12,4},{1,9},{5,13},{9,1},{13,5},{2,10},{6,14},... | collective-permute-start | bytes 884744 | tf_op jit(solution)/shard_map/ppermute | solution.py:13
  54.8 7.7 %collective-permute-done.4.rest_2_ = f32[9,32,256]{2,1,0:T(8,128)S(1)} collective-permute-done((f32[9,32,256]{2,1,0:T(8,128)S(1)}, f32[9,32,256]{2,1,0:T(8,128)S(1)}, u32[]{:S(2)}, u32[]{:S(2)}) %collective-permute-start.4) | collective-permute-done | bytes 294944 | tf_op jit(solution)/shard_map/ppermute | solution.py:13
  62.5 1.5 %collective-permute-start.21 = (f32[3,128,256]{2,1,0:T(8,128)S(1)}, f32[3,128,256]{2,1,0:T(8,128)S(1)}, u32[]{:S(2)}, u32[]{:S(2)}) collective-permute-start(f32[3,128,256]{2,1,0:T(8,128)S(1)} %pad_maximum_fusion.7.rest_1_), channel_id=1, source_target_pairs={{0,8},{4,12},{8,0},{12,4},{1,9},{5,13},{9,1},{13,5},{2,10},{6,14},... | collective-permute-start | bytes 1179656 | tf_op jit(solution)/shard_map/ppermute | solution.py:13
  64.0 4.8 %collective-permute-done.5.rest_3_ = f32[9,32,256]{2,1,0:T(8,128)S(1)} collective-permute-done((f32[9,32,256]{2,1,0:T(8,128)S(1)}, f32[9,32,256]{2,1,0:T(8,128)S(1)}, u32[]{:S(2)}, u32[]{:S(2)}) %collective-permute-start.5) | collective-permute-done | bytes 294944 | tf_op jit(solution)/shard_map/ppermute | solution.py:13
  71.2 4.2 %collective-permute-done.21.rest_3_ = f32[3,128,256]{2,1,0:T(8,128)S(1)} collective-permute-done((f32[3,128,256]{2,1,0:T(8,128)S(1)}, f32[3,128,256]{2,1,0:T(8,128)S(1)}, u32[]{:S(2)}, u32[]{:S(2)}) %collective-permute-start.21) | collective-permute-done | bytes 393248 | tf_op jit(solution)/shard_map/ppermute | solution.py:13
  77.6 9.8 %collective-permute-done.20.rest_2_ = f32[3,128,256]{2,1,0:T(8,128)S(1)} collective-permute-done((f32[3,128,256]{2,1,0:T(8,128)S(1)}, f32[3,128,256]{2,1,0:T(8,128)S(1)}, u32[]{:S(2)}, u32[]{:S(2)}) %collective-permute-start.20) | collective-permute-done | bytes 393248 | tf_op jit(solution)/shard_map/ppermute | solution.py:13
  88.9 6.9 %collective-permute-done.22.rest_4_ = f32[3,128,256]{2,1,0:T(8,128)S(1)} collective-permute-done((f32[3,128,256]{2,1,0:T(8,128)S(1)}, f32[3,128,256]{2,1,0:T(8,128)S(1)}, u32[]{:S(2)}, u32[]{:S(2)}) %collective-permute-start.22) | collective-permute-done | bytes 393248 | tf_op jit(solution)/shard_map/ppermute | solution.py:13
  97.2 2.4 %shard_map.69 = f32[512,256]{1,0:T(8,128)} custom-call(s32[3]{0:T(128)S(1)} %pad_add_fusion.place, f32[512,256]{1,0:T(8,128)S(1)} %copy-done.3, f32[3,128,256]{2,1,0:T(8,128)S(1)} %pad_maximum_fusion.7.rest_1_, f32[3,128,256]{2,1,0:T(8,128)S(1)} %collective-permute-done.20.rest_2_, f32[3,128,256]{2,1,0:T(8,128)S(1)} %collective-permute-done.21.rest_3_, ...), custom_call_target="tpu_custom_call" | custom-call | flops 805306368 | bytes 3145728 | tf_op jit(solution)/shard_map/pallas_call | solution.py:162
  100.3 2.3 %collective-permute-start.9 = (f32[128,256]{1,0:T(8,128)}, f32[128,256]{1,0:T(8,128)}, u32[]{:S(2)}, u32[]{:S(2)}) collective-permute-start(f32[128,256]{1,0:T(8,128)} %get-tuple-element.28), channel_id=1, source_target_pairs={{0,1},{1,0},{2,3},{3,2},{4,5},{5,4},{6,7},{7,6},{8,9},{9,8},{10,11... | collective-permute-start | bytes 393224 | tf_op jit(solution)/shard_map/ppermute | solution.py:13
  105.5 1.6 %collective-permute-start.15 = (f32[9,32,256]{2,1,0:T(8,128)S(1)}, f32[9,32,256]{2,1,0:T(8,128)S(1)}, u32[]{:S(2)}, u32[]{:S(2)}) collective-permute-start(f32[9,32,256]{2,1,0:T(8,128)S(1)} %pad_maximum_fusion.10.rest_0_), channel_id=1, source_target_pairs={{0,8},{4,12},{8,0},{12,4},{1,9},{5,13},{9,1},{13,5},{2,10},{6,14},... | collective-permute-start | bytes 884744 | tf_op jit(solution)/shard_map/ppermute | solution.py:13
  111.8 3.7 %collective-permute-done.15.rest_2_ = f32[9,32,256]{2,1,0:T(8,128)S(1)} collective-permute-done((f32[9,32,256]{2,1,0:T(8,128)S(1)}, f32[9,32,256]{2,1,0:T(8,128)S(1)}, u32[]{:S(2)}, u32[]{:S(2)}) %collective-permute-start.15) | collective-permute-done | bytes 294944 | tf_op jit(solution)/shard_map/ppermute | solution.py:13
  115.5 5.3 %collective-permute-done.16.rest_3_ = f32[9,32,256]{2,1,0:T(8,128)S(1)} collective-permute-done((f32[9,32,256]{2,1,0:T(8,128)}, f32[9,32,256]{2,1,0:T(8,128)S(1)}, u32[]{:S(2)}, u32[]{:S(2)}) %collective-permute-start.16) | collective-permute-done | bytes 294944 | tf_op jit(solution)/shard_map/ppermute | solution.py:13
  120.7 2.4 %shard_map.70 = f32[4,128,256]{2,1,0:T(8,128)S(1)} custom-call(s32[3]{0:T(128)S(1)} %pad_add_fusion.place, f32[2,256,1024]{2,1,0:T(8,128)S(1)} %copy-done, f32[9,32,256]{2,1,0:T(8,128)S(1)} %pad_maximum_fusion.10.rest_0_, f32[9,32,256]{2,1,0:T(8,128)} %collective-permute-done.14.rest_1_, f32[9,32,256]{2,1,0:T(8,128)S(1)} %collective-permute-done.15.rest_2_, ...), custom_call_target="tpu_custom_call" | custom-call | flops 805306368 | bytes 2228224 | tf_op jit(solution)/shard_map/pallas_call | solution.py:162
  124.7 2.9 %collective-permute-start.27 = (f32[128,256]{1,0:T(8,128)S(1)}, f32[128,256]{1,0:T(8,128)S(1)}, u32[]{:S(2)}, u32[]{:S(2)}) collective-permute-start(f32[128,256]{1,0:T(8,128)S(1)} %get-tuple-element.31), channel_id=1, source_target_pairs={{0,1},{1,0},{2,3},{3,2},{4,5},{5,4},{6,7},{7,6},{8,9},{9,8},{10,11... | collective-permute-start | bytes 393224 | tf_op jit(solution)/shard_map/ppermute | solution.py:13
  127.6 1.6 %collective-permute-start.33 = (f32[3,64,512]{2,1,0:T(8,128)S(1)}, f32[3,64,512]{2,1,0:T(8,128)S(1)}, u32[]{:S(2)}, u32[]{:S(2)}) collective-permute-start(f32[3,64,512]{2,1,0:T(8,128)S(1)} %pad_maximum_fusion.8.rest_2_), channel_id=1, source_target_pairs={{0,8},{4,12},{8,0},{12,4},{1,9},{5,13},{9,1},{13,5},{2,10},{6,14},... | collective-permute-start | bytes 1179656 | tf_op jit(solution)/shard_map/ppermute | solution.py:13
  129.2 2.1 %collective-permute-done.25 = f32[128,256]{1,0:T(8,128)S(1)} collective-permute-done((f32[128,256]{1,0:T(8,128)S(1)}, f32[128,256]{1,0:T(8,128)S(1)}, u32[]{:S(2)}, u32[]{:S(2)}) %collective-permute-start.25) | collective-permute-done | bytes 131104 | tf_op jit(solution)/shard_map/ppermute | solution.py:13
  131.4 1.5 %collective-permute-start.34 = (f32[3,64,512]{2,1,0:T(8,128)S(1)}, f32[3,64,512]{2,1,0:T(8,128)S(1)}, u32[]{:S(2)}, u32[]{:S(2)}) collective-permute-start(f32[3,64,512]{2,1,0:T(8,128)S(1)} %collective-permute-done.32.rest_3_), channel_id=1, source_target_pairs={{0,8},{4,12},{8,0},{12,4},{1,9},{5,13},{9,1},{13,5},{2,10},{6,14},... | collective-permute-start | bytes 1179656 | tf_op jit(solution)/shard_map/ppermute | solution.py:13
  132.9 3.2 %collective-permute-done.26 = f32[128,256]{1,0:T(8,128)S(1)} collective-permute-done((f32[128,256]{1,0:T(8,128)S(1)}, f32[128,256]{1,0:T(8,128)S(1)}, u32[]{:S(2)}, u32[]{:S(2)}) %collective-permute-start.26) | collective-permute-done | bytes 131104 | tf_op jit(solution)/shard_map/ppermute | solution.py:13
  138.2 1.5 %collective-permute-done.33.rest_4_ = f32[3,64,512]{2,1,0:T(8,128)S(1)} collective-permute-done((f32[3,64,512]{2,1,0:T(8,128)S(1)}, f32[3,64,512]{2,1,0:T(8,128)S(1)}, u32[]{:S(2)}, u32[]{:S(2)}) %collective-permute-start.33) | collective-permute-done | bytes 393248 | tf_op jit(solution)/shard_map/ppermute | solution.py:13
  139.7 5.7 %collective-permute-done.34.rest_5_ = f32[3,64,512]{2,1,0:T(8,128)S(1)} collective-permute-done((f32[3,64,512]{2,1,0:T(8,128)S(1)}, f32[3,64,512]{2,1,0:T(8,128)S(1)}, u32[]{:S(2)}, u32[]{:S(2)}) %collective-permute-start.34) | collective-permute-done | bytes 393248 | tf_op jit(solution)/shard_map/ppermute | solution.py:13
  145.4 2.3 %shard_map.71 = f32[256,256]{1,0:T(8,128)} custom-call(s32[3]{0:T(128)S(1)} %pad_add_fusion.place, f32[256,256]{1,0:T(8,128)S(1)} %get-tuple-element.37.rest_0_, f32[256,256]{1,0:T(8,128)S(1)} %get-tuple-element.36.rest_1_, f32[3,64,512]{2,1,0:T(8,128)S(1)} %pad_maximum_fusion.8.rest_2_, f32[3,64,512]{2,1,0:T(8,128)S(1)} %collective-permute-done.32.rest_3_, ...), custom_call_target="tpu_custom_call" | custom-call | flops 805306368 | bytes 4194304 | tf_op jit(solution)/shard_map/pallas_call | solution.py:162
  148.0 1.5 %pad_maximum_fusion = f32[2,256,1024]{2,1,0:T(8,128)} fusion(f32[1,256,1024]{2,1,0:T(8,128)S(1)} %get-tuple-element.35, f32[1,256,1024]{2,1,0:T(8,128)S(1)} %get-tuple-element.34), kind=kLoop, calls=%fused_computation | loop fusion | flops 524288 | bytes 4194304 | tf_op jit(solution)/shard_map/stack | solution.py:238
  (108 shorter events, 28.6 us)
Async XLA Ops:
  1.7 14.5 %collective-permute-start = (f32[4,32,256]{2,1,0:T(8,128)S(1)}, f32[4,32,256]{2,1,0:T(8,128)S(1)}, u32[]{:S(2)}, u32[]{:S(2)}) collective-permute-start(f32[4,32,256]{2,1,0:T(8,128)S(1)} %bitcast.77), channel_id=1, source_target_pairs={{0,3},{1,2},{2,1},{3,0},{4,7},{5,6},{6,5},{7,4},{8,11},{9,10},{10,... | collective-permute-start | bytes 393224 | tf_op jit(solution)/shard_map/ppermute | solution.py:13
  6.9 12.9 %collective-permute-start.1 = (f32[4,32,256]{2,1,0:T(8,128)S(1)}, f32[4,32,256]{2,1,0:T(8,128)S(1)}, u32[]{:S(2)}, u32[]{:S(2)}) collective-permute-start(f32[4,32,256]{2,1,0:T(8,128)S(1)} %bitcast.78), channel_id=1, source_target_pairs={{0,2},{1,3},{2,0},{3,1},{4,6},{5,7},{6,4},{7,5},{8,10},{9,11},{10,... | collective-permute-start | bytes 393224 | tf_op jit(solution)/shard_map/ppermute | solution.py:13
  6.9 15.0 %collective-permute-start.2 = (f32[4,32,256]{2,1,0:T(8,128)S(1)}, f32[4,32,256]{2,1,0:T(8,128)S(1)}, u32[]{:S(2)}, u32[]{:S(2)}) collective-permute-start(f32[4,32,256]{2,1,0:T(8,128)S(1)} %bitcast.79), channel_id=1, source_target_pairs={{0,1},{1,0},{2,3},{3,2},{4,5},{5,4},{6,7},{7,6},{8,9},{9,8},{10,11... | collective-permute-start | bytes 393224 | tf_op jit(solution)/shard_map/ppermute | solution.py:13
  8.4 32.2 %collective-permute-start.17 = (f32[128,256]{1,0:T(8,128)S(1)}, f32[128,256]{1,0:T(8,128)S(1)}, u32[]{:S(2)}, u32[]{:S(2)}) collective-permute-start(f32[128,256]{1,0:T(8,128)S(1)} %constant_dynamic-slice_fusion.1), channel_id=1, source_target_pairs={{0,1},{1,0},{2,3},{3,2},{4,5},{5,4},{6,7},{7,6},{8,9},{9,8},{10,11... | collective-permute-start | bytes 393224 | tf_op jit(solution)/shard_map/ppermute | solution.py:13
  9.9 30.8 %collective-permute-start.18 = (f32[128,256]{1,0:T(8,128)S(1)}, f32[128,256]{1,0:T(8,128)S(1)}, u32[]{:S(2)}, u32[]{:S(2)}) collective-permute-start(f32[128,256]{1,0:T(8,128)S(1)} %constant_dynamic-slice_fusion.1), channel_id=1, source_target_pairs={{0,2},{1,3},{2,0},{3,1},{4,6},{5,7},{6,4},{7,5},{8,10},{9,11},{10,... | collective-permute-start | bytes 393224 | tf_op jit(solution)/shard_map/ppermute | solution.py:13
  16.2 27.6 %collective-permute-start.19 = (f32[128,256]{1,0:T(8,128)S(1)}, f32[128,256]{1,0:T(8,128)S(1)}, u32[]{:S(2)}, u32[]{:S(2)}) collective-permute-start(f32[128,256]{1,0:T(8,128)S(1)} %constant_dynamic-slice_fusion.1), channel_id=1, source_target_pairs={{0,3},{1,2},{2,1},{3,0},{4,7},{5,6},{6,5},{7,4},{8,11},{9,10},{10,... | collective-permute-start | bytes 393224 | tf_op jit(solution)/shard_map/ppermute | solution.py:13
  19.8 8.4 %collective-permute-start.11 = (f32[4,32,256]{2,1,0:T(8,128)S(1)}, f32[4,32,256]{2,1,0:T(8,128)S(1)}, u32[]{:S(2)}, u32[]{:S(2)}) collective-permute-start(f32[4,32,256]{2,1,0:T(8,128)S(1)} %bitcast.80), channel_id=1, source_target_pairs={{0,3},{1,2},{2,1},{3,0},{4,7},{5,6},{6,5},{7,4},{8,11},{9,10},{10,... | collective-permute-start | bytes 393224 | tf_op jit(solution)/shard_map/ppermute | solution.py:13
  21.9 18.7 %collective-permute-start.12 = (f32[4,32,256]{2,1,0:T(8,128)S(1)}, f32[4,32,256]{2,1,0:T(8,128)S(1)}, u32[]{:S(2)}, u32[]{:S(2)}) collective-permute-start(f32[4,32,256]{2,1,0:T(8,128)S(1)} %bitcast.81), channel_id=1, source_target_pairs={{0,2},{1,3},{2,0},{3,1},{4,6},{5,7},{6,4},{7,5},{8,10},{9,11},{10,... | collective-permute-start | bytes 393224 | tf_op jit(solution)/shard_map/ppermute | solution.py:13
  28.2 17.1 %collective-permute-start.13 = (f32[4,32,256]{2,1,0:T(8,128)S(1)}, f32[4,32,256]{2,1,0:T(8,128)S(1)}, u32[]{:S(2)}, u32[]{:S(2)}) collective-permute-start(f32[4,32,256]{2,1,0:T(8,128)S(1)} %bitcast.82), channel_id=1, source_target_pairs={{0,1},{1,0},{2,3},{3,2},{4,5},{5,4},{6,7},{7,6},{8,9},{9,8},{10,11... | collective-permute-start | bytes 393224 | tf_op jit(solution)/shard_map/ppermute | solution.py:13
  40.6 13.6 %collective-permute-start.6 = (f32[512,256]{1,0:T(8,128)}, f32[512,256]{1,0:T(8,128)S(1)}, u32[]{:S(2)}, u32[]{:S(2)}) collective-permute-start(f32[512,256]{1,0:T(8,128)} %get-tuple-element.15), channel_id=1, source_target_pairs={{0,16},{16,0},{1,17},{17,1},{2,18},{18,2},{3,19},{19,3},{4,20},{20... | collective-permute-start | bytes 1572872 | tf_op jit(solution)/shard_map/ppermute | solution.py:13
  40.7 58.9 %collective-permute-start.29 = (f32[64,512]{1,0:T(8,128)S(1)}, f32[64,512]{1,0:T(8,128)S(1)}, u32[]{:S(2)}, u32[]{:S(2)}) collective-permute-start(f32[64,512]{1,0:T(8,128)S(1)} %bitcast.74), channel_id=1, source_target_pairs={{0,1},{1,0},{2,3},{3,2},{4,5},{5,4},{6,7},{7,6},{8,9},{9,8},{10,11... | collective-permute-start | bytes 393224 | tf_op jit(solution)/shard_map/ppermute | solution.py:13
  40.7 59.5 %collective-permute-start.30 = (f32[64,512]{1,0:T(8,128)S(1)}, f32[64,512]{1,0:T(8,128)S(1)}, u32[]{:S(2)}, u32[]{:S(2)}) collective-permute-start(f32[64,512]{1,0:T(8,128)S(1)} %bitcast.75), channel_id=1, source_target_pairs={{0,2},{1,3},{2,0},{3,1},{4,6},{5,7},{6,4},{7,5},{8,10},{9,11},{10,... | collective-permute-start | bytes 393224 | tf_op jit(solution)/shard_map/ppermute | solution.py:13
  43.8 8.9 %collective-permute-start.3 = (f32[9,32,256]{2,1,0:T(8,128)S(1)}, f32[9,32,256]{2,1,0:T(8,128)S(1)}, u32[]{:S(2)}, u32[]{:S(2)}) collective-permute-start(f32[9,32,256]{2,1,0:T(8,128)S(1)} %pad_maximum_fusion.9.rest_0_), channel_id=1, source_target_pairs={{0,4},{4,0},{8,12},{12,8},{1,5},{5,1},{9,13},{13,9},{2,6},{6,2},{1... | collective-permute-start | bytes 884744 | tf_op jit(solution)/shard_map/ppermute | solution.py:13
  45.3 57.3 %collective-permute-start.31 = (f32[64,512]{1,0:T(8,128)S(1)}, f32[64,512]{1,0:T(8,128)S(1)}, u32[]{:S(2)}, u32[]{:S(2)}) collective-permute-start(f32[64,512]{1,0:T(8,128)S(1)} %bitcast.76), channel_id=1, source_target_pairs={{0,3},{1,2},{2,1},{3,0},{4,7},{5,6},{6,5},{7,4},{8,11},{9,10},{10,... | collective-permute-start | bytes 393224 | tf_op jit(solution)/shard_map/ppermute | solution.py:13
  52.6 9.9 %collective-permute-start.4 = (f32[9,32,256]{2,1,0:T(8,128)S(1)}, f32[9,32,256]{2,1,0:T(8,128)S(1)}, u32[]{:S(2)}, u32[]{:S(2)}) collective-permute-start(f32[9,32,256]{2,1,0:T(8,128)S(1)} %pad_maximum_fusion.9.rest_0_), channel_id=1, source_target_pairs={{0,8},{4,12},{8,0},{12,4},{1,9},{5,13},{9,1},{13,5},{2,10},{6,14},... | collective-permute-start | bytes 884744 | tf_op jit(solution)/shard_map/ppermute | solution.py:13
  54.2 14.7 %collective-permute-start.5 = (f32[9,32,256]{2,1,0:T(8,128)S(1)}, f32[9,32,256]{2,1,0:T(8,128)S(1)}, u32[]{:S(2)}, u32[]{:S(2)}) collective-permute-start(f32[9,32,256]{2,1,0:T(8,128)S(1)} %collective-permute-done.3.rest_1_), channel_id=1, source_target_pairs={{0,8},{4,12},{8,0},{12,4},{1,9},{5,13},{9,1},{13,5},{2,10},{6,14},... | collective-permute-start | bytes 884744 | tf_op jit(solution)/shard_map/ppermute | solution.py:13
  62.5 12.9 %collective-permute-start.21 = (f32[3,128,256]{2,1,0:T(8,128)S(1)}, f32[3,128,256]{2,1,0:T(8,128)S(1)}, u32[]{:S(2)}, u32[]{:S(2)}) collective-permute-start(f32[3,128,256]{2,1,0:T(8,128)S(1)} %pad_maximum_fusion.7.rest_1_), channel_id=1, source_target_pairs={{0,8},{4,12},{8,0},{12,4},{1,9},{5,13},{9,1},{13,5},{2,10},{6,14},... | collective-permute-start | bytes 1179656 | tf_op jit(solution)/shard_map/ppermute | solution.py:13
  75.4 12.0 %collective-permute-start.20 = (f32[3,128,256]{2,1,0:T(8,128)S(1)}, f32[3,128,256]{2,1,0:T(8,128)S(1)}, u32[]{:S(2)}, u32[]{:S(2)}) collective-permute-start(f32[3,128,256]{2,1,0:T(8,128)S(1)} %pad_maximum_fusion.7.rest_1_), channel_id=1, source_target_pairs={{0,4},{4,0},{8,12},{12,8},{1,5},{5,1},{9,13},{13,9},{2,6},{6,2},{1... | collective-permute-start | bytes 1179656 | tf_op jit(solution)/shard_map/ppermute | solution.py:13
  76.9 18.9 %collective-permute-start.22 = (f32[3,128,256]{2,1,0:T(8,128)S(1)}, f32[3,128,256]{2,1,0:T(8,128)S(1)}, u32[]{:S(2)}, u32[]{:S(2)}) collective-permute-start(f32[3,128,256]{2,1,0:T(8,128)S(1)} %collective-permute-done.21.rest_3_), channel_id=1, source_target_pairs={{0,4},{4,0},{8,12},{12,8},{1,5},{5,1},{9,13},{13,9},{2,6},{6,2},{1... | collective-permute-start | bytes 1179656 | tf_op jit(solution)/shard_map/ppermute | solution.py:13
  87.4 18.1 %collective-permute-start.14 = (f32[9,32,256]{2,1,0:T(8,128)S(1)}, f32[9,32,256]{2,1,0:T(8,128)}, u32[]{:S(2)}, u32[]{:S(2)}) collective-permute-start(f32[9,32,256]{2,1,0:T(8,128)S(1)} %pad_maximum_fusion.10.rest_0_), channel_id=1, source_target_pairs={{0,4},{4,0},{8,12},{12,8},{1,5},{5,1},{9,13},{13,9},{2,6},{6,2},{1... | collective-permute-start | bytes 884744 | tf_op jit(solution)/shard_map/ppermute | solution.py:13
  95.8 11.3 %collective-permute-start.7 = (f32[128,256]{1,0:T(8,128)}, f32[128,256]{1,0:T(8,128)}, u32[]{:S(2)}, u32[]{:S(2)}) collective-permute-start(f32[128,256]{1,0:T(8,128)} %get-tuple-element.30), channel_id=1, source_target_pairs={{0,3},{1,2},{2,1},{3,0},{4,7},{5,6},{6,5},{7,4},{8,11},{9,10},{10,... | collective-permute-start | bytes 393224 | tf_op jit(solution)/shard_map/ppermute | solution.py:13
  99.5 9.1 %collective-permute-start.8 = (f32[128,256]{1,0:T(8,128)}, f32[128,256]{1,0:T(8,128)}, u32[]{:S(2)}, u32[]{:S(2)}) collective-permute-start(f32[128,256]{1,0:T(8,128)} %get-tuple-element.29), channel_id=1, source_target_pairs={{0,2},{1,3},{2,0},{3,1},{4,6},{5,7},{6,4},{7,5},{8,10},{9,11},{10,... | collective-permute-start | bytes 393224 | tf_op jit(solution)/shard_map/ppermute | solution.py:13
  100.3 8.8 %collective-permute-start.9 = (f32[128,256]{1,0:T(8,128)}, f32[128,256]{1,0:T(8,128)}, u32[]{:S(2)}, u32[]{:S(2)}) collective-permute-start(f32[128,256]{1,0:T(8,128)} %get-tuple-element.28), channel_id=1, source_target_pairs={{0,1},{1,0},{2,3},{3,2},{4,5},{5,4},{6,7},{7,6},{8,9},{9,8},{10,11... | collective-permute-start | bytes 393224 | tf_op jit(solution)/shard_map/ppermute | solution.py:13
  105.5 9.9 %collective-permute-start.15 = (f32[9,32,256]{2,1,0:T(8,128)S(1)}, f32[9,32,256]{2,1,0:T(8,128)S(1)}, u32[]{:S(2)}, u32[]{:S(2)}) collective-permute-start(f32[9,32,256]{2,1,0:T(8,128)S(1)} %pad_maximum_fusion.10.rest_0_), channel_id=1, source_target_pairs={{0,8},{4,12},{8,0},{12,4},{1,9},{5,13},{9,1},{13,5},{2,10},{6,14},... | collective-permute-start | bytes 884744 | tf_op jit(solution)/shard_map/ppermute | solution.py:13
  107.1 20.5 %collective-permute-start.32 = (f32[3,64,512]{2,1,0:T(8,128)S(1)}, f32[3,64,512]{2,1,0:T(8,128)S(1)}, u32[]{:S(2)}, u32[]{:S(2)}) collective-permute-start(f32[3,64,512]{2,1,0:T(8,128)S(1)} %pad_maximum_fusion.8.rest_2_), channel_id=1, source_target_pairs={{0,4},{4,0},{8,12},{12,8},{1,5},{5,1},{9,13},{13,9},{2,6},{6,2},{1... | collective-permute-start | bytes 1179656 | tf_op jit(solution)/shard_map/ppermute | solution.py:13
  108.6 12.1 %collective-permute-start.16 = (f32[9,32,256]{2,1,0:T(8,128)}, f32[9,32,256]{2,1,0:T(8,128)S(1)}, u32[]{:S(2)}, u32[]{:S(2)}) collective-permute-start(f32[9,32,256]{2,1,0:T(8,128)} %collective-permute-done.14.rest_1_), channel_id=1, source_target_pairs={{0,8},{4,12},{8,0},{12,4},{1,9},{5,13},{9,1},{13,5},{2,10},{6,14},... | collective-permute-start | bytes 884744 | tf_op jit(solution)/shard_map/ppermute | solution.py:13
  110.3 26.4 %collective-permute-start.10 = (f32[128,1024]{1,0:T(8,128)S(1)}, f32[128,1024]{1,0:T(8,128)S(1)}, u32[]{:S(2)}, u32[]{:S(2)}) collective-permute-start(f32[128,1024]{1,0:T(8,128)S(1)} %pad_maximum_fusion.5), channel_id=1, source_target_pairs={{0,16},{16,0},{1,17},{17,1},{2,18},{18,2},{3,19},{19,3},{4,20},{20... | collective-permute-start | bytes 1572872 | tf_op jit(solution)/shard_map/ppermute | solution.py:13
  124.5 11.5 %collective-permute-start.26 = (f32[128,256]{1,0:T(8,128)S(1)}, f32[128,256]{1,0:T(8,128)S(1)}, u32[]{:S(2)}, u32[]{:S(2)}) collective-permute-start(f32[128,256]{1,0:T(8,128)S(1)} %get-tuple-element.32), channel_id=1, source_target_pairs={{0,2},{1,3},{2,0},{3,1},{4,6},{5,7},{6,4},{7,5},{8,10},{9,11},{10,... | collective-permute-start | bytes 393224 | tf_op jit(solution)/shard_map/ppermute | solution.py:13
  124.7 11.4 %collective-permute-start.27 = (f32[128,256]{1,0:T(8,128)S(1)}, f32[128,256]{1,0:T(8,128)S(1)}, u32[]{:S(2)}, u32[]{:S(2)}) collective-permute-start(f32[128,256]{1,0:T(8,128)S(1)} %get-tuple-element.31), channel_id=1, source_target_pairs={{0,1},{1,0},{2,3},{3,2},{4,5},{5,4},{6,7},{7,6},{8,9},{9,8},{10,11... | collective-permute-start | bytes 393224 | tf_op jit(solution)/shard_map/ppermute | solution.py:13
  127.6 12.1 %collective-permute-start.33 = (f32[3,64,512]{2,1,0:T(8,128)S(1)}, f32[3,64,512]{2,1,0:T(8,128)S(1)}, u32[]{:S(2)}, u32[]{:S(2)}) collective-permute-start(f32[3,64,512]{2,1,0:T(8,128)S(1)} %pad_maximum_fusion.8.rest_2_), channel_id=1, source_target_pairs={{0,8},{4,12},{8,0},{12,4},{1,9},{5,13},{9,1},{13,5},{2,10},{6,14},... | collective-permute-start | bytes 1179656 | tf_op jit(solution)/shard_map/ppermute | solution.py:13
  131.4 14.0 %collective-permute-start.34 = (f32[3,64,512]{2,1,0:T(8,128)S(1)}, f32[3,64,512]{2,1,0:T(8,128)S(1)}, u32[]{:S(2)}, u32[]{:S(2)}) collective-permute-start(f32[3,64,512]{2,1,0:T(8,128)S(1)} %collective-permute-done.32.rest_3_), channel_id=1, source_target_pairs={{0,8},{4,12},{8,0},{12,4},{1,9},{5,13},{9,1},{13,5},{2,10},{6,14},... | collective-permute-start | bytes 1179656 | tf_op jit(solution)/shard_map/ppermute | solution.py:13
  136.2 11.5 %collective-permute-start.28 = (f32[128,1024]{1,0:T(8,128)S(1)}, f32[128,1024]{1,0:T(8,128)S(1)}, u32[]{:S(2)}, u32[]{:S(2)}) collective-permute-start(f32[128,1024]{1,0:T(8,128)S(1)} %pad_maximum_fusion.6), channel_id=1, source_target_pairs={{0,16},{16,0},{1,17},{17,1},{2,18},{18,2},{3,19},{19,3},{4,20},{20... | collective-permute-start | bytes 1572872 | tf_op jit(solution)/shard_map/ppermute | solution.py:13
  (16 other events, 197.0 us)

commit v3 on v2

--- a/solution.py
+++ b/solution.py
@@ -38,18 +38,15 @@
     return lax.dynamic_slice_in_dim(value, lax.axis_index(axis) * size, size, dim)
 
 
-def from_depth(part, relay):
+def from_depth(part):
     size = lax.axis_size("depth")
-    if not (relay and size == 4):
-        parts = [exchange(part, "depth", k) for k in range(1, size)]
-        return jnp.stack(parts)
-    near = exchange(part, "depth", 1)
-    across = lax.ppermute(jnp.stack([part, near]), "depth", [(1, 2), (2, 1)])
-    handed = lax.ppermute(across, "depth", [(1, 0), (2, 3)])
-    index = lax.axis_index("depth")
-    outer = (index == 0) | (index == size - 1)
-    far = [jnp.where(outer, handed[0], across[1]), jnp.where(outer, handed[1], across[0])]
-    return jnp.stack([near] + far)
+    known = {}
+    for k in range(size - 1, 0, -1):
+        if k % 2 == 0:
+            known[k] = exchange(known[k + 1], "depth", 1)
+        else:
+            known[k] = exchange(part, "depth", k)
+    return [known[k] for k in range(1, size)]
 
 
 def pack_lower(parts):
@@ -70,10 +67,9 @@
     part = own_part(own, 0, "col")
     size = lax.axis_size("depth")
     if part.shape[0] % 8:
-        return from_columns(from_depth(part, False), low_first)
+        return gather_factor(part, low_first)
     part = part.reshape(part.shape[0], size, -1).transpose(1, 0, 2)
-    parts = [exchange(part, "depth", k) for k in range(1, size)]
-    return from_columns(pack_lower(parts), low_first)
+    return from_columns(pack_lower(from_depth(part)), low_first)
 
 
 def from_columns(parts, low_first):
@@ -89,8 +85,8 @@
     return [known[k] for k in range(size)]
 
 
-def gather_factor(own, low_first, relay):
-    return from_columns(from_depth(own_part(own, 0, "col"), relay), low_first)
+def gather_factor(part, low_first):
+    return from_columns(jnp.stack(from_depth(part)), low_first)
 
 
 def halves(value):
@@ -223,9 +219,9 @@
     trail_own = [trail_factor[:, section, :] for section in range(trail_factor.shape[1])]
     trail_part = own_part(trail_factor, 0, "col").reshape(count // lax.axis_size("col"), -1)
     first_factor = gather_inverse(lower[0], True)
-    mid_factor = gather_factor(head_factor, False, False)
+    mid_factor = gather_factor(own_part(head_factor, 0, "col"), False)
     second_factor = gather_inverse(lower[1], True)
-    trail_parts = from_columns(from_depth(trail_part, False), True)
+    trail_parts = gather_factor(trail_part, True)
 
     rhs = share_rows(head_rhs[0], 0)
     first_part = solve(place, 0, inverses, first_factor, rhs)

time: 150 us -> 131 us (0.87)
  starting transfers between devices: 52.7 us -> 41.5 us
  waiting for transfers between devices: 73 us -> 66.8 us
    ppermute x36, starting transfers between devices: 52.7 us -> 41.5 us  [exchange(): return lax.ppermute(value, axis, pairs)]
    ppermute x36, waiting for transfers between devices: 73 us -> 66.8 us  [exchange(): return lax.ppermute(value, axis, pairs)]
  transfers between devices with their start and end apart: 36 -> 36, of which waited for: 16 -> 18; matrix products, arithmetic and copies ran while one was open for 7% -> 7% of each run, Pallas kernels for 6% -> 6%
where the time goes in v3:
time: 131 us
  waiting for transfers between devices  66.8 us (51%)
  starting transfers between devices  41.5 us (32%)
  Pallas kernels  8.51 us (6%)
  local copies, waits for them, and re-layouts  6.84 us (5%)
  other arithmetic  6.39 us (5%)
    ppermute x36, waiting for transfers between devices, exchange(): return lax.ppermute(value, axis, pairs)  66.8 us
    ppermute x36, starting transfers between devices, exchange(): return lax.ppermute(value, axis, pairs)  41.5 us
    pallas_call x4, Pallas kernels, call_kernel(): pl.pallas_call(kernel, out_shape=out, grid_spec=pltpu.PrefetchScalarGridS...  8.51 us
    dynamic_slice x3, local copies, waits for them, and re-layouts, own_part(): lax.dynamic_slice_in_dim(value, lax.axis_index(axis) * size, size, dim)  2.9 us
  transfers between devices with their start and end apart: 36, of which 18 were waited for; matrix products, arithmetic and copies ran while one was open for 7% of the time, Pallas kernels for 6%

profile of v3, /device:TPU:0, one launch (start us, length us, event | category | flops | bytes accessed | tf_op | source)
XLA Modules:
  0.0 131.1 jit_solution(2466859010565655865)
XLA Ops:
  1.8 5.1 %collective-permute-start = (f32[4,32,256]{2,1,0:T(8,128)S(1)}, f32[4,32,256]{2,1,0:T(8,128)S(1)}, u32[]{:S(2)}, u32[]{:S(2)}) collective-permute-start(f32[4,32,256]{2,1,0:T(8,128)S(1)} %bitcast.78), channel_id=1, source_target_pairs={{0,3},{1,2},{2,1},{3,0},{4,7},{5,6},{6,5},{7,4},{8,11},{9,10},{10,... | collective-permute-start | bytes 393224 | tf_op jit(solution)/shard_map/ppermute | solution.py:13
  10.2 2.9 %collective-permute-start.11 = (f32[4,32,256]{2,1,0:T(8,128)S(1)}, f32[4,32,256]{2,1,0:T(8,128)S(1)}, u32[]{:S(2)}, u32[]{:S(2)}) collective-permute-start(f32[4,32,256]{2,1,0:T(8,128)S(1)} %bitcast.76), channel_id=1, source_target_pairs={{0,3},{1,2},{2,1},{3,0},{4,7},{5,6},{6,5},{7,4},{8,11},{9,10},{10,... | collective-permute-start | bytes 393224 | tf_op jit(solution)/shard_map/ppermute | solution.py:13
  17.2 5.5 %collective-permute-done.11 = f32[4,32,256]{2,1,0:T(8,128)S(1)} collective-permute-done((f32[4,32,256]{2,1,0:T(8,128)S(1)}, f32[4,32,256]{2,1,0:T(8,128)S(1)}, u32[]{:S(2)}, u32[]{:S(2)}) %collective-permute-start.11) | collective-permute-done | bytes 131104 | tf_op jit(solution)/shard_map/ppermute | solution.py:13
  22.7 2.3 %collective-permute-done.1 = f32[4,32,256]{2,1,0:T(8,128)S(1)} collective-permute-done((f32[4,32,256]{2,1,0:T(8,128)S(1)}, f32[4,32,256]{2,1,0:T(8,128)S(1)}, u32[]{:S(2)}, u32[]{:S(2)}) %collective-permute-start.1) | collective-permute-done | bytes 131104 | tf_op jit(solution)/shard_map/ppermute | solution.py:13
  25.0 2.4 %collective-permute-start.12 = (f32[4,32,256]{2,1,0:T(8,128)S(1)}, f32[4,32,256]{2,1,0:T(8,128)S(1)}, u32[]{:S(2)}, u32[]{:S(2)}) collective-permute-start(f32[4,32,256]{2,1,0:T(8,128)S(1)} %collective-permute-done.11), channel_id=1, source_target_pairs={{0,1},{1,0},{2,3},{3,2},{4,5},{5,4},{6,7},{7,6},{8,9},{9,8},{10,11... | collective-permute-start | bytes 393224 | tf_op jit(solution)/shard_map/ppermute | solution.py:13
  27.7 3.6 %collective-permute-done.12 = f32[4,32,256]{2,1,0:T(8,128)S(1)} collective-permute-done((f32[4,32,256]{2,1,0:T(8,128)S(1)}, f32[4,32,256]{2,1,0:T(8,128)S(1)}, u32[]{:S(2)}, u32[]{:S(2)}) %collective-permute-start.12) | collective-permute-done | bytes 131104 | tf_op jit(solution)/shard_map/ppermute | solution.py:13
  31.2 2.5 %collective-permute-start.19 = (f32[128,256]{1,0:T(8,128)S(1)}, f32[128,256]{1,0:T(8,128)S(1)}, u32[]{:S(2)}, u32[]{:S(2)}) collective-permute-start(f32[128,256]{1,0:T(8,128)S(1)} %collective-permute-done.18), channel_id=1, source_target_pairs={{0,1},{1,0},{2,3},{3,2},{4,5},{5,4},{6,7},{7,6},{8,9},{9,8},{10,11... | collective-permute-start | bytes 393224 | tf_op jit(solution)/shard_map/ppermute | solution.py:13
  33.9 1.8 %collective-permute-done.30 = f32[64,512]{1,0:T(8,128)S(1)} collective-permute-done((f32[64,512]{1,0:T(8,128)S(1)}, f32[64,512]{1,0:T(8,128)S(1)}, u32[]{:S(2)}, u32[]{:S(2)}) %collective-permute-start.30) | collective-permute-done | bytes 131104 | tf_op jit(solution)/shard_map/ppermute | solution.py:13
  35.9 2.4 %collective-permute-done.19 = f32[128,256]{1,0:T(8,128)S(1)} collective-permute-done((f32[128,256]{1,0:T(8,128)S(1)}, f32[128,256]{1,0:T(8,128)S(1)}, u32[]{:S(2)}, u32[]{:S(2)}) %collective-permute-start.19) | collective-permute-done | bytes 131104 | tf_op jit(solution)/shard_map/ppermute | solution.py:13
  38.3 1.5 %collective-permute-start.3 = (f32[9,32,256]{2,1,0:T(8,128)S(1)}, f32[9,32,256]{2,1,0:T(8,128)S(1)}, u32[]{:S(2)}, u32[]{:S(2)}) collective-permute-start(f32[9,32,256]{2,1,0:T(8,128)S(1)} %pad_maximum_fusion.9.rest_0_), channel_id=1, source_target_pairs={{0,4},{4,0},{8,12},{12,8},{1,5},{5,1},{9,13},{13,9},{2,6},{6,2},{1... | collective-permute-start | bytes 884744 | tf_op jit(solution)/shard_map/ppermute | solution.py:13
  39.8 1.6 %collective-permute-start.4 = (f32[9,32,256]{2,1,0:T(8,128)S(1)}, f32[9,32,256]{2,1,0:T(8,128)S(1)}, u32[]{:S(2)}, u32[]{:S(2)}) collective-permute-start(f32[9,32,256]{2,1,0:T(8,128)S(1)} %pad_maximum_fusion.9.rest_0_), channel_id=1, source_target_pairs={{0,8},{4,12},{8,0},{12,4},{1,9},{5,13},{9,1},{13,5},{2,10},{6,14},... | collective-permute-start | bytes 884744 | tf_op jit(solution)/shard_map/ppermute | solution.py:13
  42.0 4.4 %collective-permute-done.3.rest_1_ = f32[9,32,256]{2,1,0:T(8,128)S(1)} collective-permute-done((f32[9,32,256]{2,1,0:T(8,128)S(1)}, f32[9,32,256]{2,1,0:T(8,128)S(1)}, u32[]{:S(2)}, u32[]{:S(2)}) %collective-permute-start.3) | collective-permute-done | bytes 294944 | tf_op jit(solution)/shard_map/ppermute | solution.py:13
  46.4 1.7 %collective-permute-start.5 = (f32[9,32,256]{2,1,0:T(8,128)S(1)}, f32[9,32,256]{2,1,0:T(8,128)S(1)}, u32[]{:S(2)}, u32[]{:S(2)}) collective-permute-start(f32[9,32,256]{2,1,0:T(8,128)S(1)} %collective-permute-done.3.rest_1_), channel_id=1, source_target_pairs={{0,8},{4,12},{8,0},{12,4},{1,9},{5,13},{9,1},{13,5},{2,10},{6,14},... | collective-permute-start | bytes 884744 | tf_op jit(solution)/shard_map/ppermute | solution.py:13
  48.2 1.5 %collective-permute-done.4.rest_2_ = f32[9,32,256]{2,1,0:T(8,128)S(1)} collective-permute-done((f32[9,32,256]{2,1,0:T(8,128)S(1)}, f32[9,32,256]{2,1,0:T(8,128)S(1)}, u32[]{:S(2)}, u32[]{:S(2)}) %collective-permute-start.4) | collective-permute-done | bytes 294944 | tf_op jit(solution)/shard_map/ppermute | solution.py:13
  50.7 8.0 %collective-permute-done.5.rest_3_ = f32[9,32,256]{2,1,0:T(8,128)S(1)} collective-permute-done((f32[9,32,256]{2,1,0:T(8,128)S(1)}, f32[9,32,256]{2,1,0:T(8,128)S(1)}, u32[]{:S(2)}, u32[]{:S(2)}) %collective-permute-start.5) | collective-permute-done | bytes 294944 | tf_op jit(solution)/shard_map/ppermute | solution.py:13
  63.3 2.4 %collective-permute-start.7 = (f32[128,256]{1,0:T(8,128)}, f32[128,256]{1,0:T(8,128)}, u32[]{:S(2)}, u32[]{:S(2)}) collective-permute-start(f32[128,256]{1,0:T(8,128)} %get-tuple-element.30), channel_id=1, source_target_pairs={{0,3},{1,2},{2,1},{3,0},{4,7},{5,6},{6,5},{7,4},{8,11},{9,10},{10,... | collective-permute-start | bytes 393224 | tf_op jit(solution)/shard_map/ppermute | solution.py:13
  65.7 13.1 %collective-permute-done.22.rest_4_ = f32[3,128,256]{2,1,0:T(8,128)S(1)} collective-permute-done((f32[3,128,256]{2,1,0:T(8,128)S(1)}, f32[3,128,256]{2,1,0:T(8,128)S(1)}, u32[]{:S(2)}, u32[]{:S(2)}) %collective-permute-start.22) | collective-permute-done | bytes 393248 | tf_op jit(solution)/shard_map/ppermute | solution.py:13
  80.0 2.4 %shard_map.69 = f32[512,256]{1,0:T(8,128)} custom-call(s32[3]{0:T(128)S(1)} %pad_add_fusion.place, f32[512,256]{1,0:T(8,128)S(1)} %copy-done.3, f32[3,128,256]{2,1,0:T(8,128)S(1)} %pad_maximum_fusion.7.rest_1_, f32[3,128,256]{2,1,0:T(8,128)S(1)} %collective-permute-done.20.rest_2_, f32[3,128,256]{2,1,0:T(8,128)S(1)} %collective-permute-done.21.rest_3_, ...), custom_call_target="tpu_custom_call" | custom-call | flops 805306368 | bytes 3145728 | tf_op jit(solution)/shard_map/pallas_call | solution.py:158
  82.4 1.8 %collective-permute-start.9 = (f32[128,256]{1,0:T(8,128)}, f32[128,256]{1,0:T(8,128)}, u32[]{:S(2)}, u32[]{:S(2)}) collective-permute-start(f32[128,256]{1,0:T(8,128)} %get-tuple-element.28), channel_id=1, source_target_pairs={{0,1},{1,0},{2,3},{3,2},{4,5},{5,4},{6,7},{7,6},{8,9},{9,8},{10,11... | collective-permute-start | bytes 393224 | tf_op jit(solution)/shard_map/ppermute | solution.py:13
  87.1 1.6 %collective-permute-start.15 = (f32[9,32,256]{2,1,0:T(8,128)S(1)}, f32[9,32,256]{2,1,0:T(8,128)S(1)}, u32[]{:S(2)}, u32[]{:S(2)}) collective-permute-start(f32[9,32,256]{2,1,0:T(8,128)S(1)} %pad_maximum_fusion.10.rest_0_), channel_id=1, source_target_pairs={{0,8},{4,12},{8,0},{12,4},{1,9},{5,13},{9,1},{13,5},{2,10},{6,14},... | collective-permute-start | bytes 884744 | tf_op jit(solution)/shard_map/ppermute | solution.py:13
  92.4 4.6 %collective-permute-done.15.rest_2_ = f32[9,32,256]{2,1,0:T(8,128)S(1)} collective-permute-done((f32[9,32,256]{2,1,0:T(8,128)S(1)}, f32[9,32,256]{2,1,0:T(8,128)S(1)}, u32[]{:S(2)}, u32[]{:S(2)}) %collective-permute-start.15) | collective-permute-done | bytes 294944 | tf_op jit(solution)/shard_map/ppermute | solution.py:13
  97.0 5.3 %collective-permute-done.16.rest_3_ = f32[9,32,256]{2,1,0:T(8,128)S(1)} collective-permute-done((f32[9,32,256]{2,1,0:T(8,128)}, f32[9,32,256]{2,1,0:T(8,128)S(1)}, u32[]{:S(2)}, u32[]{:S(2)}) %collective-permute-start.16) | collective-permute-done | bytes 294944 | tf_op jit(solution)/shard_map/ppermute | solution.py:13
  102.3 2.4 %shard_map.70 = f32[4,128,256]{2,1,0:T(8,128)S(1)} custom-call(s32[3]{0:T(128)S(1)} %pad_add_fusion.place, f32[2,256,1024]{2,1,0:T(8,128)S(1)} %copy-done, f32[9,32,256]{2,1,0:T(8,128)S(1)} %pad_maximum_fusion.10.rest_0_, f32[9,32,256]{2,1,0:T(8,128)} %collective-permute-done.14.rest_1_, f32[9,32,256]{2,1,0:T(8,128)S(1)} %collective-permute-done.15.rest_2_, ...), custom_call_target="tpu_custom_call" | custom-call | flops 805306368 | bytes 2228224 | tf_op jit(solution)/shard_map/pallas_call | solution.py:158
  104.7 2.0 %collective-permute-start.25 = (f32[128,256]{1,0:T(8,128)S(1)}, f32[128,256]{1,0:T(8,128)S(1)}, u32[]{:S(2)}, u32[]{:S(2)}) collective-permute-start(f32[128,256]{1,0:T(8,128)S(1)} %get-tuple-element.33), channel_id=1, source_target_pairs={{0,3},{1,2},{2,1},{3,0},{4,7},{5,6},{6,5},{7,4},{8,11},{9,10},{10,... | collective-permute-start | bytes 393224 | tf_op jit(solution)/shard_map/ppermute | solution.py:13
  106.8 2.3 %collective-permute-start.27 = (f32[128,256]{1,0:T(8,128)S(1)}, f32[128,256]{1,0:T(8,128)S(1)}, u32[]{:S(2)}, u32[]{:S(2)}) collective-permute-start(f32[128,256]{1,0:T(8,128)S(1)} %get-tuple-element.31), channel_id=1, source_target_pairs={{0,1},{1,0},{2,3},{3,2},{4,5},{5,4},{6,7},{7,6},{8,9},{9,8},{10,11... | collective-permute-start | bytes 393224 | tf_op jit(solution)/shard_map/ppermute | solution.py:13
  109.2 1.6 %collective-permute-start.33 = (f32[3,64,512]{2,1,0:T(8,128)S(1)}, f32[3,64,512]{2,1,0:T(8,128)S(1)}, u32[]{:S(2)}, u32[]{:S(2)}) collective-permute-start(f32[3,64,512]{2,1,0:T(8,128)S(1)} %pad_maximum_fusion.8.rest_2_), channel_id=1, source_target_pairs={{0,8},{4,12},{8,0},{12,4},{1,9},{5,13},{9,1},{13,5},{2,10},{6,14},... | collective-permute-start | bytes 1179656 | tf_op jit(solution)/shard_map/ppermute | solution.py:13
  110.8 2.2 %collective-permute-done.25 = f32[128,256]{1,0:T(8,128)S(1)} collective-permute-done((f32[128,256]{1,0:T(8,128)S(1)}, f32[128,256]{1,0:T(8,128)S(1)}, u32[]{:S(2)}, u32[]{:S(2)}) %collective-permute-start.25) | collective-permute-done | bytes 131104 | tf_op jit(solution)/shard_map/ppermute | solution.py:13
  112.9 1.5 %collective-permute-start.34 = (f32[3,64,512]{2,1,0:T(8,128)S(1)}, f32[3,64,512]{2,1,0:T(8,128)S(1)}, u32[]{:S(2)}, u32[]{:S(2)}) collective-permute-start(f32[3,64,512]{2,1,0:T(8,128)S(1)} %collective-permute-done.32.rest_3_), channel_id=1, source_target_pairs={{0,8},{4,12},{8,0},{12,4},{1,9},{5,13},{9,1},{13,5},{2,10},{6,14},... | collective-permute-start | bytes 1179656 | tf_op jit(solution)/shard_map/ppermute | solution.py:13
  114.5 3.6 %collective-permute-done.26 = f32[128,256]{1,0:T(8,128)S(1)} collective-permute-done((f32[128,256]{1,0:T(8,128)S(1)}, f32[128,256]{1,0:T(8,128)S(1)}, u32[]{:S(2)}, u32[]{:S(2)}) %collective-permute-start.26) | collective-permute-done | bytes 131104 | tf_op jit(solution)/shard_map/ppermute | solution.py:13
  121.3 5.7 %collective-permute-done.34.rest_5_ = f32[3,64,512]{2,1,0:T(8,128)S(1)} collective-permute-done((f32[3,64,512]{2,1,0:T(8,128)S(1)}, f32[3,64,512]{2,1,0:T(8,128)S(1)}, u32[]{:S(2)}, u32[]{:S(2)}) %collective-permute-start.34) | collective-permute-done | bytes 393248 | tf_op jit(solution)/shard_map/ppermute | solution.py:13
  126.9 2.4 %shard_map.71 = f32[256,256]{1,0:T(8,128)} custom-call(s32[3]{0:T(128)S(1)} %pad_add_fusion.place, f32[256,256]{1,0:T(8,128)S(1)} %get-tuple-element.37.rest_0_, f32[256,256]{1,0:T(8,128)S(1)} %get-tuple-element.36.rest_1_, f32[3,64,512]{2,1,0:T(8,128)S(1)} %pad_maximum_fusion.8.rest_2_, f32[3,64,512]{2,1,0:T(8,128)S(1)} %collective-permute-done.32.rest_3_, ...), custom_call_target="tpu_custom_call" | custom-call | flops 805306368 | bytes 4194304 | tf_op jit(solution)/shard_map/pallas_call | solution.py:158
  129.6 1.5 %pad_maximum_fusion = f32[2,256,1024]{2,1,0:T(8,128)} fusion(f32[1,256,1024]{2,1,0:T(8,128)S(1)} %get-tuple-element.35, f32[1,256,1024]{2,1,0:T(8,128)S(1)} %get-tuple-element.34), kind=kLoop, calls=%fused_computation | loop fusion | flops 524288 | bytes 4194304 | tf_op jit(solution)/shard_map/stack | solution.py:234
  (108 shorter events, 26.7 us)
Async XLA Ops:
  1.8 12.3 %collective-permute-start = (f32[4,32,256]{2,1,0:T(8,128)S(1)}, f32[4,32,256]{2,1,0:T(8,128)S(1)}, u32[]{:S(2)}, u32[]{:S(2)}) collective-permute-start(f32[4,32,256]{2,1,0:T(8,128)S(1)} %bitcast.78), channel_id=1, source_target_pairs={{0,3},{1,2},{2,1},{3,0},{4,7},{5,6},{6,5},{7,4},{8,11},{9,10},{10,... | collective-permute-start | bytes 393224 | tf_op jit(solution)/shard_map/ppermute | solution.py:13
  7.0 9.1 %collective-permute-start.2 = (f32[4,32,256]{2,1,0:T(8,128)S(1)}, f32[4,32,256]{2,1,0:T(8,128)S(1)}, u32[]{:S(2)}, u32[]{:S(2)}) collective-permute-start(f32[4,32,256]{2,1,0:T(8,128)S(1)} %bitcast.79), channel_id=1, source_target_pairs={{0,1},{1,0},{2,3},{3,2},{4,5},{5,4},{6,7},{7,6},{8,9},{9,8},{10,11... | collective-permute-start | bytes 393224 | tf_op jit(solution)/shard_map/ppermute | solution.py:13
  7.9 19.6 %collective-permute-start.18 = (f32[128,256]{1,0:T(8,128)S(1)}, f32[128,256]{1,0:T(8,128)S(1)}, u32[]{:S(2)}, u32[]{:S(2)}) collective-permute-start(f32[128,256]{1,0:T(8,128)S(1)} %constant_dynamic-slice_fusion.1), channel_id=1, source_target_pairs={{0,3},{1,2},{2,1},{3,0},{4,7},{5,6},{6,5},{7,4},{8,11},{9,10},{10,... | collective-permute-start | bytes 393224 | tf_op jit(solution)/shard_map/ppermute | solution.py:13
  8.9 24.9 %collective-permute-start.17 = (f32[128,256]{1,0:T(8,128)S(1)}, f32[128,256]{1,0:T(8,128)S(1)}, u32[]{:S(2)}, u32[]{:S(2)}) collective-permute-start(f32[128,256]{1,0:T(8,128)S(1)} %constant_dynamic-slice_fusion.1), channel_id=1, source_target_pairs={{0,1},{1,0},{2,3},{3,2},{4,5},{5,4},{6,7},{7,6},{8,9},{9,8},{10,11... | collective-permute-start | bytes 393224 | tf_op jit(solution)/shard_map/ppermute | solution.py:13
  10.2 12.5 %collective-permute-start.11 = (f32[4,32,256]{2,1,0:T(8,128)S(1)}, f32[4,32,256]{2,1,0:T(8,128)S(1)}, u32[]{:S(2)}, u32[]{:S(2)}) collective-permute-start(f32[4,32,256]{2,1,0:T(8,128)S(1)} %bitcast.76), channel_id=1, source_target_pairs={{0,3},{1,2},{2,1},{3,0},{4,7},{5,6},{6,5},{7,4},{8,11},{9,10},{10,... | collective-permute-start | bytes 393224 | tf_op jit(solution)/shard_map/ppermute | solution.py:13
  14.1 10.9 %collective-permute-start.1 = (f32[4,32,256]{2,1,0:T(8,128)S(1)}, f32[4,32,256]{2,1,0:T(8,128)S(1)}, u32[]{:S(2)}, u32[]{:S(2)}) collective-permute-start(f32[4,32,256]{2,1,0:T(8,128)S(1)} %collective-permute-done), channel_id=1, source_target_pairs={{0,1},{1,0},{2,3},{3,2},{4,5},{5,4},{6,7},{7,6},{8,9},{9,8},{10,11... | collective-permute-start | bytes 393224 | tf_op jit(solution)/shard_map/ppermute | solution.py:13
  16.1 23.7 %collective-permute-start.13 = (f32[4,32,256]{2,1,0:T(8,128)S(1)}, f32[4,32,256]{2,1,0:T(8,128)S(1)}, u32[]{:S(2)}, u32[]{:S(2)}) collective-permute-start(f32[4,32,256]{2,1,0:T(8,128)S(1)} %bitcast.77), channel_id=1, source_target_pairs={{0,1},{1,0},{2,3},{3,2},{4,5},{5,4},{6,7},{7,6},{8,9},{9,8},{10,11... | collective-permute-start | bytes 393224 | tf_op jit(solution)/shard_map/ppermute | solution.py:13
  22.7 18.7 %collective-permute-start.6 = (f32[512,256]{1,0:T(8,128)}, f32[512,256]{1,0:T(8,128)S(1)}, u32[]{:S(2)}, u32[]{:S(2)}) collective-permute-start(f32[512,256]{1,0:T(8,128)} %get-tuple-element.15), channel_id=1, source_target_pairs={{0,16},{16,0},{1,17},{17,1},{2,18},{18,2},{3,19},{19,3},{4,20},{20... | collective-permute-start | bytes 1572872 | tf_op jit(solution)/shard_map/ppermute | solution.py:13
  27.5 8.2 %collective-permute-start.30 = (f32[64,512]{1,0:T(8,128)S(1)}, f32[64,512]{1,0:T(8,128)S(1)}, u32[]{:S(2)}, u32[]{:S(2)}) collective-permute-start(f32[64,512]{1,0:T(8,128)S(1)} %bitcast.74), channel_id=1, source_target_pairs={{0,3},{1,2},{2,1},{3,0},{4,7},{5,6},{6,5},{7,4},{8,11},{9,10},{10,... | collective-permute-start | bytes 393224 | tf_op jit(solution)/shard_map/ppermute | solution.py:13
  31.2 7.0 %collective-permute-start.19 = (f32[128,256]{1,0:T(8,128)S(1)}, f32[128,256]{1,0:T(8,128)S(1)}, u32[]{:S(2)}, u32[]{:S(2)}) collective-permute-start(f32[128,256]{1,0:T(8,128)S(1)} %collective-permute-done.18), channel_id=1, source_target_pairs={{0,1},{1,0},{2,3},{3,2},{4,5},{5,4},{6,7},{7,6},{8,9},{9,8},{10,11... | collective-permute-start | bytes 393224 | tf_op jit(solution)/shard_map/ppermute | solution.py:13
  33.8 48.6 %collective-permute-start.29 = (f32[64,512]{1,0:T(8,128)S(1)}, f32[64,512]{1,0:T(8,128)S(1)}, u32[]{:S(2)}, u32[]{:S(2)}) collective-permute-start(f32[64,512]{1,0:T(8,128)S(1)} %bitcast.75), channel_id=1, source_target_pairs={{0,1},{1,0},{2,3},{3,2},{4,5},{5,4},{6,7},{7,6},{8,9},{9,8},{10,11... | collective-permute-start | bytes 393224 | tf_op jit(solution)/shard_map/ppermute | solution.py:13
  35.7 48.4 %collective-permute-start.31 = (f32[64,512]{1,0:T(8,128)S(1)}, f32[64,512]{1,0:T(8,128)S(1)}, u32[]{:S(2)}, u32[]{:S(2)}) collective-permute-start(f32[64,512]{1,0:T(8,128)S(1)} %collective-permute-done.30), channel_id=1, source_target_pairs={{0,1},{1,0},{2,3},{3,2},{4,5},{5,4},{6,7},{7,6},{8,9},{9,8},{10,11... | collective-permute-start | bytes 393224 | tf_op jit(solution)/shard_map/ppermute | solution.py:13
  38.3 8.1 %collective-permute-start.3 = (f32[9,32,256]{2,1,0:T(8,128)S(1)}, f32[9,32,256]{2,1,0:T(8,128)S(1)}, u32[]{:S(2)}, u32[]{:S(2)}) collective-permute-start(f32[9,32,256]{2,1,0:T(8,128)S(1)} %pad_maximum_fusion.9.rest_0_), channel_id=1, source_target_pairs={{0,4},{4,0},{8,12},{12,8},{1,5},{5,1},{9,13},{13,9},{2,6},{6,2},{1... | collective-permute-start | bytes 884744 | tf_op jit(solution)/shard_map/ppermute | solution.py:13
  39.8 9.9 %collective-permute-start.4 = (f32[9,32,256]{2,1,0:T(8,128)S(1)}, f32[9,32,256]{2,1,0:T(8,128)S(1)}, u32[]{:S(2)}, u32[]{:S(2)}) collective-permute-start(f32[9,32,256]{2,1,0:T(8,128)S(1)} %pad_maximum_fusion.9.rest_0_), channel_id=1, source_target_pairs={{0,8},{4,12},{8,0},{12,4},{1,9},{5,13},{9,1},{13,5},{2,10},{6,14},... | collective-permute-start | bytes 884744 | tf_op jit(solution)/shard_map/ppermute | solution.py:13
  41.4 19.6 %collective-permute-start.21 = (f32[3,128,256]{2,1,0:T(8,128)S(1)}, f32[3,128,256]{2,1,0:T(8,128)S(1)}, u32[]{:S(2)}, u32[]{:S(2)}) collective-permute-start(f32[3,128,256]{2,1,0:T(8,128)S(1)} %pad_maximum_fusion.7.rest_1_), channel_id=1, source_target_pairs={{0,8},{4,12},{8,0},{12,4},{1,9},{5,13},{9,1},{13,5},{2,10},{6,14},... | collective-permute-start | bytes 1179656 | tf_op jit(solution)/shard_map/ppermute | solution.py:13
  46.4 12.2 %collective-permute-start.5 = (f32[9,32,256]{2,1,0:T(8,128)S(1)}, f32[9,32,256]{2,1,0:T(8,128)S(1)}, u32[]{:S(2)}, u32[]{:S(2)}) collective-permute-start(f32[9,32,256]{2,1,0:T(8,128)S(1)} %collective-permute-done.3.rest_1_), channel_id=1, source_target_pairs={{0,8},{4,12},{8,0},{12,4},{1,9},{5,13},{9,1},{13,5},{2,10},{6,14},... | collective-permute-start | bytes 884744 | tf_op jit(solution)/shard_map/ppermute | solution.py:13
  49.8 13.6 %collective-permute-start.20 = (f32[3,128,256]{2,1,0:T(8,128)S(1)}, f32[3,128,256]{2,1,0:T(8,128)S(1)}, u32[]{:S(2)}, u32[]{:S(2)}) collective-permute-start(f32[3,128,256]{2,1,0:T(8,128)S(1)} %pad_maximum_fusion.7.rest_1_), channel_id=1, source_target_pairs={{0,4},{4,0},{8,12},{12,8},{1,5},{5,1},{9,13},{13,9},{2,6},{6,2},{1... | collective-permute-start | bytes 1179656 | tf_op jit(solution)/shard_map/ppermute | solution.py:13
  61.0 26.0 %collective-permute-start.14 = (f32[9,32,256]{2,1,0:T(8,128)S(1)}, f32[9,32,256]{2,1,0:T(8,128)}, u32[]{:S(2)}, u32[]{:S(2)}) collective-permute-start(f32[9,32,256]{2,1,0:T(8,128)S(1)} %pad_maximum_fusion.10.rest_0_), channel_id=1, source_target_pairs={{0,4},{4,0},{8,12},{12,8},{1,5},{5,1},{9,13},{13,9},{2,6},{6,2},{1... | collective-permute-start | bytes 884744 | tf_op jit(solution)/shard_map/ppermute | solution.py:13
  62.0 16.8 %collective-permute-start.22 = (f32[3,128,256]{2,1,0:T(8,128)S(1)}, f32[3,128,256]{2,1,0:T(8,128)S(1)}, u32[]{:S(2)}, u32[]{:S(2)}) collective-permute-start(f32[3,128,256]{2,1,0:T(8,128)S(1)} %collective-permute-done.21.rest_3_), channel_id=1, source_target_pairs={{0,4},{4,0},{8,12},{12,8},{1,5},{5,1},{9,13},{13,9},{2,6},{6,2},{1... | collective-permute-start | bytes 1179656 | tf_op jit(solution)/shard_map/ppermute | solution.py:13
  63.3 25.3 %collective-permute-start.7 = (f32[128,256]{1,0:T(8,128)}, f32[128,256]{1,0:T(8,128)}, u32[]{:S(2)}, u32[]{:S(2)}) collective-permute-start(f32[128,256]{1,0:T(8,128)} %get-tuple-element.30), channel_id=1, source_target_pairs={{0,3},{1,2},{2,1},{3,0},{4,7},{5,6},{6,5},{7,4},{8,11},{9,10},{10,... | collective-permute-start | bytes 393224 | tf_op jit(solution)/shard_map/ppermute | solution.py:13
  78.9 10.3 %collective-permute-start.8 = (f32[128,256]{1,0:T(8,128)}, f32[128,256]{1,0:T(8,128)}, u32[]{:S(2)}, u32[]{:S(2)}) collective-permute-start(f32[128,256]{1,0:T(8,128)} %get-tuple-element.29), channel_id=1, source_target_pairs={{0,2},{1,3},{2,0},{3,1},{4,6},{5,7},{6,4},{7,5},{8,10},{9,11},{10,... | collective-permute-start | bytes 393224 | tf_op jit(solution)/shard_map/ppermute | solution.py:13
  82.4 7.3 %collective-permute-start.9 = (f32[128,256]{1,0:T(8,128)}, f32[128,256]{1,0:T(8,128)}, u32[]{:S(2)}, u32[]{:S(2)}) collective-permute-start(f32[128,256]{1,0:T(8,128)} %get-tuple-element.28), channel_id=1, source_target_pairs={{0,1},{1,0},{2,3},{3,2},{4,5},{5,4},{6,7},{7,6},{8,9},{9,8},{10,11... | collective-permute-start | bytes 393224 | tf_op jit(solution)/shard_map/ppermute | solution.py:13
  87.1 9.9 %collective-permute-start.15 = (f32[9,32,256]{2,1,0:T(8,128)S(1)}, f32[9,32,256]{2,1,0:T(8,128)S(1)}, u32[]{:S(2)}, u32[]{:S(2)}) collective-permute-start(f32[9,32,256]{2,1,0:T(8,128)S(1)} %pad_maximum_fusion.10.rest_0_), channel_id=1, source_target_pairs={{0,8},{4,12},{8,0},{12,4},{1,9},{5,13},{9,1},{13,5},{2,10},{6,14},... | collective-permute-start | bytes 884744 | tf_op jit(solution)/shard_map/ppermute | solution.py:13
  88.7 20.5 %collective-permute-start.32 = (f32[3,64,512]{2,1,0:T(8,128)S(1)}, f32[3,64,512]{2,1,0:T(8,128)S(1)}, u32[]{:S(2)}, u32[]{:S(2)}) collective-permute-start(f32[3,64,512]{2,1,0:T(8,128)S(1)} %pad_maximum_fusion.8.rest_2_), channel_id=1, source_target_pairs={{0,4},{4,0},{8,12},{12,8},{1,5},{5,1},{9,13},{13,9},{2,6},{6,2},{1... | collective-permute-start | bytes 1179656 | tf_op jit(solution)/shard_map/ppermute | solution.py:13
  89.2 13.1 %collective-permute-start.16 = (f32[9,32,256]{2,1,0:T(8,128)}, f32[9,32,256]{2,1,0:T(8,128)S(1)}, u32[]{:S(2)}, u32[]{:S(2)}) collective-permute-start(f32[9,32,256]{2,1,0:T(8,128)} %collective-permute-done.14.rest_1_), channel_id=1, source_target_pairs={{0,8},{4,12},{8,0},{12,4},{1,9},{5,13},{9,1},{13,5},{2,10},{6,14},... | collective-permute-start | bytes 884744 | tf_op jit(solution)/shard_map/ppermute | solution.py:13
  90.9 27.8 %collective-permute-start.10 = (f32[128,1024]{1,0:T(8,128)S(1)}, f32[128,1024]{1,0:T(8,128)S(1)}, u32[]{:S(2)}, u32[]{:S(2)}) collective-permute-start(f32[128,1024]{1,0:T(8,128)S(1)} %pad_maximum_fusion.5), channel_id=1, source_target_pairs={{0,16},{16,0},{1,17},{17,1},{2,18},{18,2},{3,19},{19,3},{4,20},{20... | collective-permute-start | bytes 1572872 | tf_op jit(solution)/shard_map/ppermute | solution.py:13
  104.7 8.3 %collective-permute-start.25 = (f32[128,256]{1,0:T(8,128)S(1)}, f32[128,256]{1,0:T(8,128)S(1)}, u32[]{:S(2)}, u32[]{:S(2)}) collective-permute-start(f32[128,256]{1,0:T(8,128)S(1)} %get-tuple-element.33), channel_id=1, source_target_pairs={{0,3},{1,2},{2,1},{3,0},{4,7},{5,6},{6,5},{7,4},{8,11},{9,10},{10,... | collective-permute-start | bytes 393224 | tf_op jit(solution)/shard_map/ppermute | solution.py:13
  106.7 11.3 %collective-permute-start.26 = (f32[128,256]{1,0:T(8,128)S(1)}, f32[128,256]{1,0:T(8,128)S(1)}, u32[]{:S(2)}, u32[]{:S(2)}) collective-permute-start(f32[128,256]{1,0:T(8,128)S(1)} %get-tuple-element.32), channel_id=1, source_target_pairs={{0,2},{1,3},{2,0},{3,1},{4,6},{5,7},{6,4},{7,5},{8,10},{9,11},{10,... | collective-permute-start | bytes 393224 | tf_op jit(solution)/shard_map/ppermute | solution.py:13
  106.8 11.2 %collective-permute-start.27 = (f32[128,256]{1,0:T(8,128)S(1)}, f32[128,256]{1,0:T(8,128)S(1)}, u32[]{:S(2)}, u32[]{:S(2)}) collective-permute-start(f32[128,256]{1,0:T(8,128)S(1)} %get-tuple-element.31), channel_id=1, source_target_pairs={{0,1},{1,0},{2,3},{3,2},{4,5},{5,4},{6,7},{7,6},{8,9},{9,8},{10,11... | collective-permute-start | bytes 393224 | tf_op jit(solution)/shard_map/ppermute | solution.py:13
  109.2 12.1 %collective-permute-start.33 = (f32[3,64,512]{2,1,0:T(8,128)S(1)}, f32[3,64,512]{2,1,0:T(8,128)S(1)}, u32[]{:S(2)}, u32[]{:S(2)}) collective-permute-start(f32[3,64,512]{2,1,0:T(8,128)S(1)} %pad_maximum_fusion.8.rest_2_), channel_id=1, source_target_pairs={{0,8},{4,12},{8,0},{12,4},{1,9},{5,13},{9,1},{13,5},{2,10},{6,14},... | collective-permute-start | bytes 1179656 | tf_op jit(solution)/shard_map/ppermute | solution.py:13
  112.9 14.0 %collective-permute-start.34 = (f32[3,64,512]{2,1,0:T(8,128)S(1)}, f32[3,64,512]{2,1,0:T(8,128)S(1)}, u32[]{:S(2)}, u32[]{:S(2)}) collective-permute-start(f32[3,64,512]{2,1,0:T(8,128)S(1)} %collective-permute-done.32.rest_3_), channel_id=1, source_target_pairs={{0,8},{4,12},{8,0},{12,4},{1,9},{5,13},{9,1},{13,5},{2,10},{6,14},... | collective-permute-start | bytes 1179656 | tf_op jit(solution)/shard_map/ppermute | solution.py:13
  118.2 11.1 %collective-permute-start.28 = (f32[128,1024]{1,0:T(8,128)S(1)}, f32[128,1024]{1,0:T(8,128)S(1)}, u32[]{:S(2)}, u32[]{:S(2)}) collective-permute-start(f32[128,1024]{1,0:T(8,128)S(1)} %pad_maximum_fusion.6), channel_id=1, source_target_pairs={{0,16},{16,0},{1,17},{17,1},{2,18},{18,2},{3,19},{19,3},{4,20},{20... | collective-permute-start | bytes 1572872 | tf_op jit(solution)/shard_map/ppermute | solution.py:13
  (16 other events, 149.3 us)
